TPU v7x, 32 devices: a whole 2x2x4 slice. The times are simulated.
32 devices in a mesh: dp: 2 (over core), row: 4 (over y, x), col: 4 (over z).
Axes of the slice: x: 2, y: 2, z: 4, core: 2. Of those that a mesh axis runs over, the one named last changes fastest.
Arguments:
- tokens: bfloat16 [1024, 768], P(('dp', 'col'), 'row'), may hold values from -150 to 150
- out_grad: bfloat16 [1024, 768], P(('dp', 'col'), 'row'), may hold values from -6 to 6
- segment_ids: int32 [2, 512], P('dp'), may hold values from 0 to 1, never falling along the last dimension, each value on 1 to 384 neighbouring positions
- w_qkv: bfloat16 [768, 2304], P('row', 'col'), may hold values from -8 to 8
- w_out: bfloat16 [768, 768], P('col', 'row'), may hold values from -0.875 to 0.875
- w_fc: bfloat16 [768, 3072], P('row', 'col'), may hold values from -0.21875 to 0.21875
- w_proj: bfloat16 [3072, 768], P('col', 'row'), may hold values from -0.109375 to 0.109375
- bias_qkv: float32 [2304], P('col'), may hold values from -1.8 to 1.8
- bias_fc: float32 [3072], P('col'), may hold values from -1.8 to 1.8
- row_vectors: float32 [6, 768], P(None, 'row'), may hold values from -0.6 to 1.5
- mom_qkv: float32 [768, 2304], P('row', 'col'), may hold values from -20 to 20
- mom_out: float32 [768, 768], P('col', 'row'), may hold values from -20 to 20
- mom_fc: float32 [768, 3072], P('row', 'col'), may hold values from -20 to 20
- mom_proj: float32 [3072, 768], P('col', 'row'), may hold values from -20 to 20
- mom_bias_qkv: float32 [2304], P('col'), may hold values from -20 to 20
- mom_bias_fc: float32 [3072], P('col'), may hold values from -20 to 20
- mom_rows: float32 [6, 768], P(None, 'row'), may hold values from -20 to 20
Outputs:
- block_out: bfloat16 [1024, 768], P(('dp', 'col'), 'row')
- input_grad: float32 [1024, 768], P(('dp', 'col'), 'row')
- grad_qkv: float32 [768, 2304], P('row', 'col')
- grad_out: float32 [768, 768], P('col', 'row')
- grad_fc: float32 [768, 3072], P('row', 'col')
- grad_proj: float32 [3072, 768], P('col', 'row')
- grad_bias_qkv: float32 [2304], P('col')
- grad_bias_fc: float32 [3072], P('col')
- grad_rows: float32 [6, 768], P(None, 'row')
- new_qkv: float32 [768, 2304], P('row', 'col')
- new_out: float32 [768, 768], P('col', 'row')
- new_fc: float32 [768, 3072], P('row', 'col')
- new_proj: float32 [3072, 768], P('col', 'row')
- new_bias_qkv: float32 [2304], P('col')
- new_bias_fc: float32 [3072], P('col')
- new_rows: float32 [6, 768], P(None, 'row')
- new_mom_qkv: float32 [768, 2304], P('row', 'col')
- new_mom_out: float32 [768, 768], P('col', 'row')
- new_mom_fc: float32 [768, 3072], P('row', 'col')
- new_mom_proj: float32 [3072, 768], P('col', 'row')
- new_mom_bias_qkv: float32 [2304], P('col')
- new_mom_bias_fc: float32 [3072], P('col')
- new_mom_rows: float32 [6, 768], P(None, 'row')
Inputs may be any that keep to these rules, and one draw needn't show every extreme that they name: `segment_ids`: within each data group the segment numbers never fall; the group's 2 sequences have 512 tokens together, each at most 384.
All inputs are finite; a program needn't handle non-finite values.
Results may differ from a plain program's by a relative error of at most 0.012.
Values may be sent and summed in bfloat16 or wider, within the bound.
A program may use at most 128 MiB of HBM per device.

v0:
```python
import math

import jax
import jax.numpy as jnp
from jax import lax
from jax.sharding import PartitionSpec as P

HD = 64
TOK_G = 512
NS_STEPS = 2


eps_norm = 1e-05
eps_gram = 1e-06
coef_a = 3.4445
coef_b = -4.775
coef_c = 2.0315
beta_mom = 0.95
rate_matrix = 0.03
rate_vector = 0.6


def as_sent(array):

    def short(part):
        return part.astype(jnp.bfloat16) if part.dtype == jnp.float32 else part

    return jax.tree.map(short, array)


def gelu_value(values):
    return jax.nn.gelu(values, approximate=True)


def gelu_slope(values):
    return jax.vjp(gelu_value, values)[1](jnp.ones_like(values))[0]


def product(left_side, right_side, flip_right):
    if flip_right:
        return lax.dot_general(
            left_side, right_side, (((1,), (1,)), ((), ())), preferred_element_type=jnp.float32
        )
    return jnp.dot(left_side, right_side, preferred_element_type=jnp.float32)


def inner_rows(left_side, right_side):
    return lax.dot_general(
        left_side, right_side, (((0,), (0,)), ((), ())), preferred_element_type=jnp.float32
    )


def feature_sums(first_term, second_term):
    return lax.psum(
        (jnp.sum(first_term, axis=1, keepdims=True), jnp.sum(second_term, axis=1, keepdims=True)),
        "row",
    )


def norm_forward(values, gain_row, shift_row):
    feature_count = values.shape[1] * lax.axis_size("row")
    total_sum, square_sum = feature_sums(values, values * values)
    mean_row = total_sum / feature_count
    inv_std = lax.rsqrt(square_sum / feature_count - mean_row * mean_row + eps_norm)
    unit_rows = (values - mean_row) * inv_std
    return (unit_rows, inv_std, unit_rows * gain_row + shift_row)


def norm_backward(grad_rows, unit_rows, inv_std, gain_row):
    feature_count = grad_rows.shape[1] * lax.axis_size("row")
    scaled = grad_rows * gain_row
    first_sum, second_sum = feature_sums(scaled, scaled * unit_rows)
    return inv_std * (scaled - first_sum / feature_count - unit_rows * (second_sum / feature_count))


def tokens_over_col(local_piece):
    return lax.all_gather(local_piece, "col", axis=0, tiled=True)


def tokens_over_row(local_piece):
    return lax.all_gather(local_piece, "row", axis=0, tiled=True)


def reduce_to_row(whole_rows, weight, flip_right):
    own_rows = whole_rows.shape[0] // lax.axis_size("row")

    def term_rows(row_start, row_count):
        return product(whole_rows, weight, flip_right)

    return lax.psum_scatter(
        term_rows(jnp.int32(0), own_rows * lax.axis_size("row")),
        "row",
        scatter_dimension=0,
        tiled=True,
    )


def reduce_to_col(whole_rows, weight, flip_right):
    own_rows = whole_rows.shape[0] // lax.axis_size("col")

    def term_rows(row_start, row_count):
        return product(whole_rows, weight, flip_right)

    return lax.psum_scatter(
        term_rows(jnp.int32(0), own_rows * lax.axis_size("col")),
        "col",
        scatter_dimension=0,
        tiled=True,
    )


def attend_block(query_rows, key_rows, value_rows, allowed, score_scale):
    scores = (
        jnp.einsum("qhe,khe->hqk", query_rows, key_rows, preferred_element_type=jnp.float32)
        * score_scale
    )
    scores = jnp.where(allowed[None], scores, -jnp.inf)
    row_max = jnp.max(scores, axis=2, keepdims=True)
    log_total = row_max + jnp.log(jnp.sum(jnp.exp(scores - row_max), axis=2, keepdims=True))
    prob_low = jnp.exp(scores - log_total).astype(jnp.bfloat16)
    attended = jnp.einsum("hqk,khe->qhe", prob_low, value_rows, preferred_element_type=jnp.float32)
    return (attended.astype(jnp.bfloat16), log_total)


def attend_grad(
    query_rows, key_rows, value_rows, allowed, score_scale, grad_low, attended, log_total
):
    scores = (
        jnp.einsum("qhe,khe->hqk", query_rows, key_rows, preferred_element_type=jnp.float32)
        * score_scale
    )
    scores = jnp.where(allowed[None], scores, -jnp.inf)
    probs_full = jnp.exp(scores - log_total)
    prob_low = probs_full.astype(jnp.bfloat16)
    grad_value = jnp.einsum("hqk,qhe->khe", prob_low, grad_low, preferred_element_type=jnp.float32)
    grad_probs = jnp.einsum(
        "qhe,khe->hqk", grad_low, value_rows, preferred_element_type=jnp.float32
    )
    row_dot = jnp.sum(grad_low.astype(jnp.float32) * attended.astype(jnp.float32), axis=2).T[
        :, :, None
    ]
    grad_scores = (score_scale * probs_full * (grad_probs - row_dot)).astype(jnp.bfloat16)
    grad_query = jnp.einsum(
        "hqk,khe->qhe", grad_scores, key_rows, preferred_element_type=jnp.float32
    )
    grad_key = jnp.einsum(
        "hqk,qhe->khe", grad_scores, query_rows, preferred_element_type=jnp.float32
    )
    return (grad_query, grad_key, grad_value)


def query_layout(query_rows, segment_row, row_base):
    row_count = query_rows.shape[0]
    block_rows = row_count // max(1, row_count // 512)
    block_count = row_count // block_rows
    positions = (row_base + jnp.arange(row_count, dtype=jnp.int32)).reshape(block_count, block_rows)
    query_segments = lax.dynamic_slice_in_dim(segment_row, row_base, row_count, 0).reshape(
        block_count, block_rows
    )
    return (block_count, block_rows, positions, query_segments)


def allowed_pairs(position_part, segment_part, segment_row):
    key_positions = jnp.arange(segment_row.shape[0], dtype=jnp.int32)
    return (key_positions[None, :] <= position_part[:, None]) & (
        segment_row[None, :] == segment_part[:, None]
    )


def attention_forward(query_rows, key_rows, value_rows, segment_row, row_base, score_scale):
    block_count, block_rows, positions, query_segments = query_layout(
        query_rows, segment_row, row_base
    )
    query_parts = query_rows.reshape(
        block_count, block_rows, query_rows.shape[1], query_rows.shape[2]
    )

    def one_block(inputs):
        query_part, position_part, segment_part = inputs
        return attend_block(
            query_part,
            key_rows,
            value_rows,
            allowed_pairs(position_part, segment_part, segment_row),
            score_scale,
        )

    attended, log_total = lax.map(one_block, (query_parts, positions, query_segments))
    return (attended.reshape(query_rows.shape), log_total)


def attention_backward(
    query_rows,
    key_rows,
    value_rows,
    segment_row,
    row_base,
    score_scale,
    grad_low,
    attended,
    log_total,
):
    block_count, block_rows, positions, query_segments = query_layout(
        query_rows, segment_row, row_base
    )
    block_shape = (block_count, block_rows, query_rows.shape[1], query_rows.shape[2])

    def one_block(carry, inputs):
        query_part, position_part, segment_part, grad_part, attended_part, total_part = inputs
        allowed = allowed_pairs(position_part, segment_part, segment_row)
        grad_query, grad_key, grad_value = attend_grad(
            query_part,
            key_rows,
            value_rows,
            allowed,
            score_scale,
            grad_part,
            attended_part,
            total_part,
        )
        return ((carry[0] + grad_key, carry[1] + grad_value), grad_query)

    start_carry = (jnp.zeros(key_rows.shape, jnp.float32), jnp.zeros(value_rows.shape, jnp.float32))
    sums, grad_query = lax.scan(
        one_block,
        start_carry,
        (
            query_rows.reshape(block_shape),
            positions,
            query_segments,
            grad_low.reshape(block_shape),
            attended.reshape(block_shape),
            log_total,
        ),
    )
    return (grad_query.reshape(query_rows.shape), sums[0], sums[1])


def orthogonalize(update_low):
    flipped = update_low.shape[0] > update_low.shape[1]
    matrix = update_low.T if flipped else update_low
    gram_matrix = jnp.dot(matrix, matrix.T, preferred_element_type=jnp.float32)
    gram_norm = jnp.sqrt(jnp.sum(gram_matrix * gram_matrix)) + eps_gram
    current = (matrix.astype(jnp.float32) / jnp.sqrt(gram_norm)).astype(jnp.bfloat16)
    gram_low = (gram_matrix / gram_norm).astype(jnp.bfloat16)
    for repeat in range(NS_STEPS):
        if repeat > 0:
            gram_low = jnp.dot(current, current.T, preferred_element_type=jnp.float32).astype(
                jnp.bfloat16
            )
        polynomial = (
            coef_b * gram_low.astype(jnp.float32)
            + coef_c * jnp.dot(gram_low, gram_low, preferred_element_type=jnp.float32)
        ).astype(jnp.bfloat16)
        current = (
            coef_a * current.astype(jnp.float32)
            + jnp.dot(polynomial, current, preferred_element_type=jnp.float32)
        ).astype(jnp.bfloat16)
    return current.T if flipped else current


def assemble(blocks, colrow, row_parts, col_parts):
    height = blocks.shape[1]
    breadth = blocks.shape[2]
    tiled = blocks.reshape(row_parts, col_parts, height, breadth)
    if colrow:
        return tiled.transpose(1, 2, 0, 3).reshape(col_parts * height, row_parts * breadth)
    return tiled.transpose(0, 2, 1, 3).reshape(row_parts * height, col_parts * breadth)


def split_blocks(whole_matrix, colrow, row_parts, col_parts):
    if colrow:
        height = whole_matrix.shape[0] // col_parts
        breadth = whole_matrix.shape[1] // row_parts
        tiled = whole_matrix.reshape(col_parts, height, row_parts, breadth)
        return tiled.transpose(2, 0, 1, 3).reshape(row_parts * col_parts, height, breadth)
    height = whole_matrix.shape[0] // row_parts
    breadth = whole_matrix.shape[1] // col_parts
    tiled = whole_matrix.reshape(row_parts, height, col_parts, breadth)
    return tiled.transpose(0, 2, 1, 3).reshape(row_parts * col_parts, height, breadth)


def local(
    tokens,
    out_grad,
    segment_ids,
    w_qkv,
    w_out,
    w_fc,
    w_proj,
    bias_qkv,
    bias_fc,
    row_vectors,
    mom_qkv,
    mom_out,
    mom_fc,
    mom_proj,
    mom_bias_qkv,
    mom_bias_fc,
    mom_rows,
):
    score_scale = 1.0 / math.sqrt(HD)
    row_parts = lax.axis_size("row")
    col_parts = lax.axis_size("col")
    segment_row = segment_ids[0]
    query_count = segment_row.shape[0] // row_parts
    row_base = lax.axis_index("row") * query_count
    gain_one = row_vectors[0]
    shift_one = row_vectors[1]
    gain_two = row_vectors[2]
    shift_two = row_vectors[3]
    bias_out = row_vectors[4]
    bias_proj = row_vectors[5]
    resid_in = tokens.astype(jnp.float32)
    unit_one, inv_one, normed_one = norm_forward(resid_in, gain_one, shift_one)
    act_one = tokens_over_col(normed_one.astype(jnp.bfloat16))
    qkv_local = (reduce_to_row(act_one, w_qkv, False) + bias_qkv).astype(jnp.bfloat16)
    heads_local = qkv_local.shape[1] // (3 * HD)
    qkv_tiles = qkv_local.reshape(query_count, heads_local, 3, HD)
    pair_local = qkv_tiles[:, :, 1:].reshape(query_count, heads_local * 2 * HD)
    pair_all = lax.all_gather(pair_local, "row", axis=0, tiled=True).reshape(-1, heads_local, 2, HD)
    key_rows = pair_all[:, :, 0]
    value_rows = pair_all[:, :, 1]
    query_rows = qkv_tiles[:, :, 0]
    attended, log_total = attention_forward(
        query_rows, key_rows, value_rows, segment_row, row_base, score_scale
    )
    attn_all = tokens_over_row(attended.reshape(query_count, heads_local * HD))
    resid_mid = resid_in + reduce_to_col(attn_all, w_out, False) + bias_out
    unit_two, inv_two, normed_two = norm_forward(resid_mid, gain_two, shift_two)
    act_two = tokens_over_col(normed_two.astype(jnp.bfloat16))
    hidden_pre = reduce_to_row(act_two, w_fc, False) + bias_fc
    hidden_all = tokens_over_row(gelu_value(hidden_pre).astype(jnp.bfloat16))
    block_out = (resid_mid + reduce_to_col(hidden_all, w_proj, False) + bias_proj).astype(
        jnp.bfloat16
    )
    grad_all = tokens_over_col(out_grad)
    grad_hidden = reduce_to_row(grad_all, w_proj, True)
    grad_pre_all = tokens_over_row((gelu_slope(hidden_pre) * grad_hidden).astype(jnp.bfloat16))
    grad_w_proj = inner_rows(hidden_all, grad_all)
    grad_w_fc = inner_rows(act_two, grad_pre_all)
    grad_b_fc = jnp.sum(grad_pre_all, axis=0, dtype=jnp.float32)
    grad_norm_two = reduce_to_col(grad_pre_all, w_fc, True)
    grad_mid = out_grad.astype(jnp.float32) + norm_backward(
        grad_norm_two, unit_two, inv_two, gain_two
    )
    grad_mid_low = grad_mid.astype(jnp.bfloat16)
    grad_mid_all = tokens_over_col(grad_mid_low)
    grad_w_out = inner_rows(attn_all, grad_mid_all)
    grad_attn = (
        reduce_to_row(grad_mid_all, w_out, True)
        .astype(jnp.bfloat16)
        .reshape(query_count, heads_local, HD)
    )
    grad_query, grad_key, grad_value = attention_backward(
        query_rows,
        key_rows,
        value_rows,
        segment_row,
        row_base,
        score_scale,
        grad_attn,
        attended,
        log_total,
    )
    pair_grad = lax.psum_scatter(
        jnp.stack([grad_key, grad_value], axis=2)
        .reshape(grad_key.shape[0], heads_local * 2 * HD)
        .astype(jnp.bfloat16),
        "row",
        scatter_dimension=0,
        tiled=True,
    ).astype(jnp.float32)
    grad_qkv_local = (
        jnp.concatenate(
            [grad_query[:, :, None], pair_grad.reshape(query_count, heads_local, 2, HD)], axis=2
        )
        .reshape(query_count, heads_local * 3 * HD)
        .astype(jnp.bfloat16)
    )
    grad_qkv_all = tokens_over_row(grad_qkv_local)
    grad_w_qkv = inner_rows(act_one, grad_qkv_all)
    grad_b_qkv = jnp.sum(grad_qkv_all, axis=0, dtype=jnp.float32)
    grad_norm_one = reduce_to_col(grad_qkv_all, w_qkv, True)
    input_grad = grad_mid + norm_backward(grad_norm_one, unit_one, inv_one, gain_one)
    row_terms = jnp.stack(
        [
            jnp.sum(grad_norm_one * unit_one, axis=0),
            jnp.sum(grad_norm_one, axis=0),
            jnp.sum(grad_norm_two * unit_two, axis=0),
            jnp.sum(grad_norm_two, axis=0),
            jnp.sum(grad_mid_low, axis=0, dtype=jnp.float32),
            jnp.sum(out_grad, axis=0, dtype=jnp.float32),
        ]
    )
    summed = (
        lax.psum(grad_w_qkv.astype(jnp.bfloat16), "dp").astype(jnp.float32),
        lax.psum(grad_w_out.astype(jnp.bfloat16), "dp").astype(jnp.float32),
        lax.psum(grad_w_fc.astype(jnp.bfloat16), "dp").astype(jnp.float32),
        lax.psum(grad_w_proj.astype(jnp.bfloat16), "dp").astype(jnp.float32),
        lax.psum(grad_b_qkv.astype(jnp.bfloat16), "dp").astype(jnp.float32),
        lax.psum(grad_b_fc.astype(jnp.bfloat16), "dp").astype(jnp.float32),
    )
    grad_rows = lax.psum(row_terms, ("dp", "col"))
    weights = (w_qkv, w_out, w_fc, w_proj)
    moments = (mom_qkv, mom_out, mom_fc, mom_proj)
    new_moms = [beta_mom * moments[member] + summed[member] for member in range(4)]
    pushes = [
        (summed[member] + beta_mom * new_moms[member]).astype(jnp.bfloat16) for member in range(4)
    ]
    colrow = (False, True, False, True)
    slot_count = row_parts * col_parts
    sizes_flat = [pushed.size for pushed in pushes]
    widest = max(sizes_flat)
    owner_slots = [member * slot_count // 4 for member in range(4)]
    flat_index = lax.axis_index("row") * col_parts + lax.axis_index("col")
    branch_id = jnp.zeros((), jnp.int32)
    for member in range(4):
        branch_id = branch_id + jnp.where(flat_index == owner_slots[member], member + 1, 0).astype(
            jnp.int32
        )
    outgoing = jnp.zeros((slot_count, widest), jnp.bfloat16)
    for member in range(4):
        outgoing = outgoing.at[owner_slots[member], : sizes_flat[member]].set(
            pushes[member].reshape(-1)
        )
    arrived = lax.all_to_all(outgoing, ("row", "col"), split_axis=0, concat_axis=0, tiled=True)

    def direct_work(owned_index):

        def compute(incoming):
            blocks = incoming[:, : sizes_flat[owned_index]].reshape(
                (slot_count,) + pushes[owned_index].shape
            )
            ortho_whole = orthogonalize(assemble(blocks, colrow[owned_index], row_parts, col_parts))
            part_rows = split_blocks(
                ortho_whole, colrow[owned_index], row_parts, col_parts
            ).reshape(slot_count, sizes_flat[owned_index])
            return jnp.pad(part_rows, ((0, 0), (0, widest - sizes_flat[owned_index])))

        return compute

    def nothing_sent(incoming):
        return jnp.zeros_like(incoming)

    outgoing_back = lax.switch(
        branch_id, [nothing_sent] + [direct_work(owned_index) for owned_index in range(4)], arrived
    )
    returned = jax.tree.map(
        lambda part, own: part.astype(own.dtype),
        lax.all_to_all(
            as_sent(outgoing_back), ("row", "col"), split_axis=0, concat_axis=0, tiled=True
        ),
        outgoing_back,
    )
    orthos = [
        returned[owner_slots[member], : sizes_flat[member]].reshape(pushes[member].shape)
        for member in range(4)
    ]
    new_weights = []
    for member in range(4):
        block_shape = weights[member].shape
        if colrow[member]:
            longest = max(block_shape[0] * col_parts, block_shape[1] * row_parts)
        else:
            longest = max(block_shape[0] * row_parts, block_shape[1] * col_parts)
        new_weights.append(
            weights[member].astype(jnp.float32)
            - rate_matrix * math.sqrt(longest) * orthos[member].astype(jnp.float32)
        )
    vector_rate = rate_vector / math.sqrt(TOK_G * lax.axis_size("dp"))

    def vector_step(weight, gradient, moment):
        new_moment = beta_mom * moment + gradient
        return (weight - vector_rate * (gradient + beta_mom * new_moment), new_moment)

    new_bias_qkv, new_mom_bias_qkv = vector_step(bias_qkv, summed[4], mom_bias_qkv)
    new_bias_fc, new_mom_bias_fc = vector_step(bias_fc, summed[5], mom_bias_fc)
    new_rows, new_mom_rows = vector_step(row_vectors, grad_rows, mom_rows)
    return (
        block_out,
        input_grad,
        summed[0],
        summed[1],
        summed[2],
        summed[3],
        summed[4],
        summed[5],
        grad_rows,
        new_weights[0],
        new_weights[1],
        new_weights[2],
        new_weights[3],
        new_bias_qkv,
        new_bias_fc,
        new_rows,
        new_moms[0],
        new_moms[1],
        new_moms[2],
        new_moms[3],
        new_mom_bias_qkv,
        new_mom_bias_fc,
        new_mom_rows,
    )


def solution(mesh):
    placed = (
        P(("dp", "col"), "row"),
        P(("dp", "col"), "row"),
        P("dp", None),
        P("row", "col"),
        P("col", "row"),
        P("row", "col"),
        P("col", "row"),
        P("col"),
        P("col"),
        P(None, "row"),
        P("row", "col"),
        P("col", "row"),
        P("row", "col"),
        P("col", "row"),
        P("col"),
        P("col"),
        P(None, "row"),
    )
    return jax.shard_map(
        local,
        mesh=mesh,
        in_specs=placed,
        out_specs=(
            P(("dp", "col"), "row"),
            P(("dp", "col"), "row"),
            P("row", "col"),
            P("col", "row"),
            P("row", "col"),
            P("col", "row"),
            P("col"),
            P("col"),
            P(None, "row"),
            P("row", "col"),
            P("col", "row"),
            P("row", "col"),
            P("col", "row"),
            P("col"),
            P("col"),
            P(None, "row"),
            P("row", "col"),
            P("col", "row"),
            P("row", "col"),
            P("col", "row"),
            P("col"),
            P("col"),
            P(None, "row"),
        ),
        check_vma=False,
    )
```

profile of v0, /device:TPU:0, one launch (start us, length us, event | category | flops | bytes accessed | tf_op | source)
XLA Modules:
  0.0 831.3 jit_solution(6296389199950604514)
XLA Ops:
  9.6 11.4 %all-reduce.6 = (f32[128,1]{0,1:T(1,128)S(1)}, f32[128,1]{0,1:T(1,128)S(1)}) all-reduce(f32[128,1]{0,1:T(1,128)S(1)} %bitcast.275, f32[128,1]{0,1:T(1,128)S(1)} %bitcast.274), channel_id=1, replica_groups=mesh['dp'=2,'row'=4,'col'=4] {'row'}, use_global_device_ids=true, to_apply=%region_3.0 | all-reduce | flops 256 | bytes 2048 | tf_op jit(solution)/shard_map/psum | solution.py:54
  21.9 13.1 %all_gather.27 = bf16[512,192]{0,1:T(8,128)(2,1)S(1)} all-gather(bf16[128,192]{0,1:T(8,128)(2,1)S(1)} %fusion.64), channel_id=1, replica_groups=mesh['dp'=2,'row'=4,'col'=4] {'col'}, dimensions={0}, use_global_device_ids=true | all-gather | bytes 245760 | tf_op jit(solution)/shard_map/all_gather | solution.py:77
  37.6 26.2 %reduce-scatter.12.cloned.1.call-done = f32[128,576]{0,1:T(8,128)} async-done(((f32[512,576]{0,1:T(8,128)}), f32[128,576]{0,1:T(8,128)}) %reduce-scatter.12.cloned.1.call-update) | async-done | bytes 294928 | tf_op jit(solution)/shard_map/reduce_scatter | solution.py:90
  65.0 9.7 %all_gather.28 = bf16[512,384]{0,1:T(8,128)(2,1)S(1)} all-gather(bf16[128,384]{0,1:T(8,128)(2,1)S(1)} %bitcast.248), channel_id=1, replica_groups=mesh['dp'=2,'row'=4,'col'=4] {'row'}, dimensions={0}, use_global_device_ids=true | all-gather | bytes 491520 | tf_op jit(solution)/shard_map/all_gather | solution.py:321
  75.8 7.7 all_gather.29
  84.6 14.1 %all_gather.32 = bf16[512,192]{0,1:T(8,128)(2,1)S(1)} all-gather(bf16[128,192]{0,1:T(8,128)(2,1)S(1)} %copy-done.25), channel_id=1, replica_groups=mesh['dp'=2,'row'=4,'col'=4] {'col'}, dimensions={0}, use_global_device_ids=true | all-gather | bytes 245760 | tf_op jit(solution)/shard_map/all_gather | solution.py:77
  100.3 5.4 reduce-scatter.14.cloned.1.call-done
  106.7 10.2 %all-reduce.5 = (f32[128,1]{0,1:T(1,128)S(1)}, f32[128,1]{0,1:T(1,128)S(1)}) all-reduce(f32[128,1]{0,1:T(1,128)S(1)} %bitcast.269, f32[128,1]{0,1:T(1,128)S(1)} %bitcast.268), channel_id=1, replica_groups=mesh['dp'=2,'row'=4,'col'=4] {'row'}, use_global_device_ids=true, to_apply=%region_11.12 | all-reduce | flops 256 | bytes 2048 | tf_op jit(solution)/shard_map/psum | solution.py:54
  117.0 12.5 %all_gather.30 = bf16[512,192]{0,1:T(8,128)(2,1)S(1)} all-gather(bf16[128,192]{0,1:T(8,128)(2,1)S(1)} %add_convert_fusion.21), channel_id=1, replica_groups=mesh['dp'=2,'row'=4,'col'=4] {'col'}, dimensions={0}, use_global_device_ids=true | all-gather | bytes 245760 | tf_op jit(solution)/shard_map/all_gather | solution.py:77
  131.2 7.2 reduce-scatter.20.cloned.1.call-done
  138.4 34.0 %reduce-scatter.16.cloned.1.call-done = f32[128,768]{1,0:T(8,128)} async-done(((f32[512,768]{1,0:T(8,128)}), f32[128,768]{1,0:T(8,128)}) %reduce-scatter.16.cloned.1.call-update) | async-done | bytes 393232 | tf_op jit(solution)/shard_map/reduce_scatter | solution.py:90
  174.4 11.1 %all_gather.33 = bf16[512,768]{1,0:T(8,128)(2,1)S(1)} all-gather(bf16[128,768]{1,0:T(8,128)(2,1)S(1)} %get-tuple-element.279), channel_id=1, replica_groups=mesh['dp'=2,'row'=4,'col'=4] {'row'}, dimensions={0}, use_global_device_ids=true | all-gather | bytes 983040 | tf_op jit(solution)/shard_map/all_gather | solution.py:81
  186.8 20.8 %reduce-scatter.22.cloned.1.call-done = f32[128,192]{0,1:T(8,128)} async-done(((f32[512,192]{0,1:T(8,128)}), f32[128,192]{0,1:T(8,128)}) %reduce-scatter.22.cloned.1.call-update) | async-done | bytes 98320 | tf_op jit(solution)/shard_map/reduce_scatter | solution.py:104
  209.2 9.8 %all-reduce.4 = (f32[128,1]{0,1:T(1,128)S(1)}, f32[128,1]{0,1:T(1,128)S(1)}) all-reduce(f32[128,1]{0,1:T(1,128)S(1)} %bitcast.270, f32[128,1]{0,1:T(1,128)S(1)} %bitcast.271), channel_id=1, replica_groups=mesh['dp'=2,'row'=4,'col'=4] {'row'}, use_global_device_ids=true, to_apply=%region_19.20 | all-reduce | flops 256 | bytes 2048 | tf_op jit(solution)/shard_map/psum | solution.py:54
  220.8 12.6 %all_gather.34 = bf16[512,192]{0,1:T(8,128)(2,1)S(1)} all-gather(bf16[128,192]{0,1:T(8,128)(2,1)S(1)} %get-tuple-element.269), channel_id=1, replica_groups=mesh['dp'=2,'row'=4,'col'=4] {'col'}, dimensions={0}, use_global_device_ids=true | all-gather | bytes 245760 | tf_op jit(solution)/shard_map/all_gather | solution.py:77
  234.4 21.5 %reduce-scatter.24.cloned.1.call-done = f32[128,192]{0,1:T(8,128)} async-done(((f32[512,192]{0,1:T(8,128)}), f32[128,192]{0,1:T(8,128)}) %reduce-scatter.24.cloned.1.call-update) | async-done | bytes 98320 | tf_op jit(solution)/shard_map/reduce_scatter | solution.py:90
  260.7 12.5 %all_gather.31 = bf16[512,768]{1,0:T(8,128)(2,1)S(1)} all-gather(bf16[128,768]{1,0:T(8,128)(2,1)S(1)} %copy-done.20), channel_id=1, replica_groups=mesh['dp'=2,'row'=4,'col'=4] {'row'}, dimensions={0}, use_global_device_ids=true | all-gather | bytes 983040 | tf_op jit(solution)/shard_map/all_gather | solution.py:81
  276.2 8.7 %reduce-scatter.28.cloned.1.call-done = bf16[128,384]{1,0:T(8,128)(2,1)} async-done(((bf16[512,384]{1,0:T(8,128)(2,1)}), bf16[128,384]{1,0:T(8,128)(2,1)}) %reduce-scatter.28.cloned.1.call-update) | async-done | bytes 98320
  285.9 11.3 %all_gather.35 = bf16[512,576]{0,1:T(8,128)(2,1)S(1)} all-gather(bf16[128,576]{0,1:T(8,128)(2,1)S(1)} %bitcast.245), channel_id=1, replica_groups=mesh['dp'=2,'row'=4,'col'=4] {'row'}, dimensions={0}, use_global_device_ids=true | all-gather | bytes 737280 | tf_op jit(solution)/shard_map/all_gather | solution.py:81
  299.1 19.2 %all-reduce.11.cloned.1.call-done = (bf16[192,576]{1,0:T(8,128)(2,1)}, bf16[192,192]{1,0:T(8,128)(2,1)}, bf16[192,768]{1,0:T(8,128)(2,1)}, bf16[768,192]{0,1:T(8,128)(2,1)}) async-done(((bf16[192,576]{1,0:T(8,128)(2,1)}, bf16[192,192]{1,0:T(8,128)(2,1)}, bf16[192,768]{1,0:T(8,128)(2,1)}, bf16[768,192]{0,1:T(8,128)(2,1)}), (bf16[192,576]{1,0:T(8,128)(2,1)}, bf16[192,192]{1,0:T(8,128)(2,1)}, ...) | async-done | bytes 884752 | tf_op jit(solution)/shard_map/psum | solution.py:397
  331.4 11.5 %scatter.16 = bf16[16,1,147456]{2,0,1:T(8,128)(2,1)} dynamic-update-slice(bf16[16,1,147456]{2,0,1:T(8,128)(2,1)} %scatter.15, bf16[1,1,147456]{2,0,1:T(2,128)(2,1)S(1)} %bitcast.235, s32[]{:T(128)} %constant.270.clone.1, s32[]{:T(128)} %constant.256.clone.1, s32[]{:T(128)} %constant.256.clone.1) | dynamic-update-slice | bytes 589828 | tf_op jit(solution)/shard_map/scatter | solution.py:424
  342.9 11.5 %scatter.19 = bf16[16,1,147456]{2,0,1:T(8,128)(2,1)} dynamic-update-slice(bf16[16,1,147456]{2,0,1:T(8,128)(2,1)} %scatter.16, bf16[1,1,147456]{2,0,1:T(2,128)(2,1)S(1)} %bitcast.236, s32[]{:T(128)} %constant.272.clone.1, s32[]{:T(128)} %constant.256.clone.1, s32[]{:T(128)} %constant.256.clone.1) | dynamic-update-slice | bytes 589828 | tf_op jit(solution)/shard_map/scatter | solution.py:424
  354.9 6.8 reduce.27
  361.7 7.3 reshape.365
  368.9 6.9 all-to-all-start
  375.9 111.1 %all-to-all-done = bf16[16,2,73728]{2,1,0:T(2,128)(2,1)} async-done(((bf16[16,2,73728]{2,1,0:T(2,128)(2,1)}), bf16[16,2,73728]{2,1,0:T(2,128)(2,1)}, u32[]{:S(2)}, u32[]{:S(2)}) %all-to-all-start) | async-done | bytes 4718624 | tf_op jit(solution)/shard_map/all_to_all | solution.py:427
  486.9 12.9 %reshape.366 = bf16[16,1,147456]{2,1,0:T(2,128)(2,1)} reshape(bf16[16,2,73728]{2,1,0:T(2,128)(2,1)} %all-to-all-done) | data formatting | bytes 9437184
  499.8 87.8 %conditional.1 = (bf16[16,147456]{1,0:T(8,128)(2,1)}) conditional(s32[]{:T(128)} %clamp.3, () %tuple.43, bf16[16,1,147456]{2,1,0:T(2,128)(2,1)} %reshape.366, bf16[16,1,147456]{2,1,0:T(2,128)(2,1)} %reshape.366, bf16[16,1,147456]{2,1,0:T(2,128)(2,1)} %reshape.366, bf16[16,1,147456]{2,1,0:T(2,128)(2,1)} %reshape.366), branch_computations={%region_43.44_spmd, %region_44.46_spmd, %region_46.48_spmd, %regio... | conditional | flops 16383541248 | bytes 143917120 | solution.py:446
  500.2 9.7 %copy.138 = bf16[16,1,147456]{2,0,1:T(8,128)(2,1)S(1)} copy(bf16[16,1,147456]{2,1,0:T(2,128)(2,1)} %param.9) | data formatting | bytes 9437184 | tf_op jit(solution)/shard_map/all_to_all
  510.1 5.8 reshape.313
  516.0 7.0 copy.139
  523.0 6.6 reshape.314
  529.6 4.9 multiply_reduce_fusion
  535.3 9.1 %add_convert_fusion.1 = bf16[768,2304]{1,0:T(8,128)(2,1)} fusion(bf16[768,2304]{1,0:T(8,128)(2,1)S(1)} %reshape.314, f32[]{:T(128)S(6)} %sqrt.17, f32[768,768]{1,0:T(8,128)} %get-tuple-element.272, f32[]{:T(128)S(6)} %add.221), kind=kOutput, calls=%fused_computation.1 | convolution fusion | flops 3646881792 | bytes 9437192 | tf_op jit(solution)/shard_map/cond/branch_1_fun/dot_general | solution.py:257
  544.4 7.1 convolution_convert_fusion
  551.4 8.3 %add_convert_fusion = bf16[768,2304]{1,0:T(8,128)(2,1)S(1)} fusion(bf16[768,2304]{1,0:T(8,128)(2,1)} %add_convert_fusion.1, bf16[768,768]{1,0:T(8,128)(2,1)} %convolution_convert_fusion), kind=kOutput, calls=%fused_computation | convolution fusion | flops 3633905664 | bytes 8257536 | tf_op jit(solution)/shard_map/cond/branch_1_fun/dot_general | solution.py:257
  559.8 5.6 reshape.315
  570.0 6.1 reshape.316
  587.6 6.8 reduce.28
  594.4 7.3 reshape.367
  601.7 57.7 %all-to-all-start.1 = ((bf16[16,2,73728]{2,1,0:T(2,128)(2,1)}), bf16[16,2,73728]{2,1,0:T(2,128)(2,1)}, u32[]{:S(2)}, u32[]{:S(2)}) async-start(bf16[16,2,73728]{2,1,0:T(2,128)(2,1)} %reshape.367), calls=%async_computation.9 | async-start | bytes 9437184 | tf_op jit(solution)/shard_map/all_to_all | solution.py:451
  666.3 59.5 %reduce-scatter.26.cloned.1.call-done = f32[128,192]{0,1:T(8,128)} async-done(((f32[512,192]{0,1:T(8,128)}), f32[128,192]{0,1:T(8,128)}) %reduce-scatter.26.cloned.1.call-update) | async-done | bytes 98320 | tf_op jit(solution)/shard_map/reduce_scatter | solution.py:104
  726.9 7.5 all-reduce.3
  734.4 14.7 %reduce-scatter.18.cloned.1.call-done = f32[128,192]{0,1:T(8,128)} async-done(((f32[512,192]{0,1:T(8,128)}), f32[128,192]{0,1:T(8,128)}) %reduce-scatter.18.cloned.1.call-update) | async-done | bytes 98320 | tf_op jit(solution)/shard_map/reduce_scatter | solution.py:104
  751.0 35.8 %psum.119 = f32[6,192]{1,0:T(8,128)S(1)} all-reduce(f32[6,192]{1,0:T(8,128)S(1)} %stack.42), channel_id=1, replica_groups=mesh['dp'=2,'row'=4,'col'=4] {'dp','col'}, use_global_device_ids=true, to_apply=%region_42.43 | all-reduce | flops 1152 | bytes 9216 | tf_op jit(solution)/shard_map/psum | solution.py:404
  787.5 12.9 %reshape.368 = bf16[16,1,147456]{2,1,0:T(2,128)(2,1)} reshape(bf16[16,2,73728]{2,1,0:T(2,128)(2,1)} %all-to-all-done.1) | data formatting | bytes 9437184
  800.4 9.7 %copy.142 = bf16[16,1,147456]{2,0,1:T(8,128)(2,1)S(1)} copy(bf16[16,1,147456]{2,1,0:T(2,128)(2,1)} %reshape.368) | data formatting | bytes 9437184
  811.8 8.4 %fusion.40 = (f32[147456]{0:T(1024)S(1)}, f32[147456]{0:T(1024)S(1)}) fusion(bf16[16,1,147456]{2,1,0:T(2,128)(2,1)} %reshape.368), kind=kLoop, calls=%fused_computation.89 | loop fusion | flops 589824 | bytes 1769472 | tf_op jit(solution)/shard_map/mul | solution.py:469
  (220 shorter events, 69.9 us)
Async XLA Ops:
  7.2 30.3 %copy-start.60 = (s32[1,512]{1,0:T(1,128)S(1)}, s32[1,512]{1,0:T(1,128)}, u32[]{:S(2)}) copy-start(s32[1,512]{1,0:T(1,128)} %param.32) | copy-start | bytes 6148
  7.2 56.6 %copy-start.37 = (f32[576]{0:T(1024)S(1)}, f32[576]{0:T(1024)}, u32[]{:S(2)}) copy-start(f32[576]{0:T(1024)} %param.37) | copy-start | bytes 6916
  7.2 56.6 %reduce-scatter.12.cloned.1.call-start = ((), (), s32[]{:S(2)}) async-start(), calls=%async_computation.11 | async-start | bytes 1474560 | tf_op jit(solution)/shard_map/reduce_scatter | solution.py:90
  8.7 56.2 %copy-start.35 = (f32[1,192]{1,0:T(1,128)}, f32[1,192]{1,0:T(1,128)S(1)}, u32[]{:S(2)}) copy-start(f32[1,192]{1,0:T(1,128)S(1)} %get-tuple-element.289) | copy-start | bytes 2308
  8.7 210.4 %copy-start.32 = (f32[1,192]{1,0:T(1,128)}, f32[1,192]{1,0:T(1,128)S(1)}, u32[]{:S(2)}) copy-start(f32[1,192]{1,0:T(1,128)S(1)} %get-tuple-element.286) | copy-start | bytes 2308
  21.0 44.0 %copy-start.45 = (f32[128]{0:T(128)}, f32[128]{0:T(128)S(1)}, u32[]{:S(2)}) copy-start(f32[128]{0:T(128)S(1)} %get-tuple-element.292) | copy-start | bytes 1540
  21.0 44.0 %copy-start.47 = (f32[128]{0:T(128)}, f32[128]{0:T(128)S(1)}, u32[]{:S(2)}) copy-start(f32[128]{0:T(128)S(1)} %get-tuple-element.293) | copy-start | bytes 1540
  37.4 46.1 %copy-start.18 = (bf16[192,192]{1,0:T(8,128)(2,1)S(1)}, bf16[192,192]{1,0:T(8,128)(2,1)}, u32[]{:S(2)}) copy-start(bf16[192,192]{1,0:T(8,128)(2,1)} %param.34) | copy-start | bytes 221188
  37.4 68.3 %reduce-scatter.14.cloned.1.call-start = ((), (), s32[]{:S(2)}) async-start(), calls=%async_computation.12 | async-start | bytes 491520 | tf_op jit(solution)/shard_map/reduce_scatter | solution.py:104
  74.7 23.9 %copy-start.8 = (bf16[768,192]{0,1:T(8,128)(2,1)S(1)}, bf16[768,192]{0,1:T(8,128)(2,1)}, u32[]{:S(2)}) copy-start(bf16[768,192]{0,1:T(8,128)(2,1)} %param.36) | copy-start | bytes 884740
  84.5 45.0 %copy-start.10 = (bf16[192,768]{1,0:T(8,128)(2,1)S(1)}, bf16[192,768]{1,0:T(8,128)(2,1)}, u32[]{:S(2)}) copy-start(bf16[192,768]{1,0:T(8,128)(2,1)} %param.35) | copy-start | bytes 884740
  84.5 53.8 %reduce-scatter.20.cloned.1.call-start = ((), (), s32[]{:S(2)}) async-start(), calls=%async_computation.15 | async-start | bytes 1966080 | tf_op jit(solution)/shard_map/reduce_scatter | solution.py:90
  100.2 72.1 %copy-start.39 = (f32[768]{0:T(1024)S(1)}, f32[768]{0:T(1024)}, u32[]{:S(2)}) copy-start(f32[768]{0:T(1024)} %param.38) | copy-start | bytes 9220
  100.3 72.1 %reduce-scatter.16.cloned.1.call-start = ((), (), s32[]{:S(2)}) async-start(), calls=%async_computation.13 | async-start | bytes 1966080 | tf_op jit(solution)/shard_map/reduce_scatter | solution.py:90
  106.7 112.4 %copy-start.12 = (f32[128,192]{0,1:T(8,128)}, f32[128,192]{0,1:T(8,128)S(1)}, u32[]{:S(2)}) copy-start(f32[128,192]{0,1:T(8,128)S(1)} %get-tuple-element.270) | copy-start | bytes 294916
  116.9 102.3 %copy-start.41 = (f32[128]{0:T(128)}, f32[128]{0:T(128)S(1)}, u32[]{:S(2)}) copy-start(f32[128]{0:T(128)S(1)} %get-tuple-element.290) | copy-start | bytes 1540
  116.9 102.3 %copy-start.43 = (f32[128]{0:T(128)}, f32[128]{0:T(128)S(1)}, u32[]{:S(2)}) copy-start(f32[128]{0:T(128)S(1)} %get-tuple-element.291) | copy-start | bytes 1540
  131.1 76.5 %reduce-scatter.22.cloned.1.call-start = ((), (), s32[]{:S(2)}) async-start(), calls=%async_computation.16 | async-start | bytes 491520 | tf_op jit(solution)/shard_map/reduce_scatter | solution.py:104
  185.5 74.1 %copy-start = (bf16[512,768]{1,0:T(8,128)(2,1)}, bf16[512,768]{1,0:T(8,128)(2,1)S(1)}, u32[]{:S(2)}) copy-start(bf16[512,768]{1,0:T(8,128)(2,1)S(1)} %all_gather.33) | copy-start | bytes 2359300
  186.7 69.1 %reduce-scatter.24.cloned.1.call-start = ((), (), s32[]{:S(2)}) async-start(), calls=%async_computation.17 | async-start | bytes 491520 | tf_op jit(solution)/shard_map/reduce_scatter | solution.py:90
  234.3 50.5 %reduce-scatter.28.cloned.1.call-start = ((), (), s32[]{:S(2)}) async-start(), calls=%async_computation.19 | async-start | bytes 491520
  259.6 58.8 %all-reduce.11.cloned.1.call-start = ((), (), s32[]{:S(2)}) async-start(), calls=%async_computation.20 | async-start | bytes 1867776 | tf_op jit(solution)/shard_map/psum | solution.py:397
  275.1 43.2 %copy-start.24 = (f32[192,576]{1,0:T(8,128)S(1)}, f32[192,576]{1,0:T(8,128)}, u32[]{:S(2)}) copy-start(f32[192,576]{1,0:T(8,128)} %param.40) | copy-start | bytes 1327108
  368.9 118.0 %all-to-all-start = ((bf16[16,2,73728]{2,1,0:T(2,128)(2,1)}), bf16[16,2,73728]{2,1,0:T(2,128)(2,1)}, u32[]{:S(2)}, u32[]{:S(2)}) async-start(bf16[16,2,73728]{2,1,0:T(2,128)(2,1)} %reshape.365), calls=%async_computation.8 | async-start | bytes 9437184 | tf_op jit(solution)/shard_map/all_to_all | solution.py:427
  601.7 57.8 %copy-start.3 = (bf16[512,576]{0,1:T(8,128)(2,1)S(1)}, bf16[512,576]{0,1:T(8,128)(2,1)}, u32[]{:S(2)}) copy-start(bf16[512,576]{0,1:T(8,128)(2,1)} %copy-done.2) | copy-start | bytes 1769476
  601.7 57.8 %copy-start.14 = (bf16[192,576]{1,0:T(8,128)(2,1)S(1)}, bf16[192,576]{1,0:T(8,128)(2,1)}, u32[]{:S(2)}) copy-start(bf16[192,576]{1,0:T(8,128)(2,1)} %param.33) | copy-start | bytes 663556
  601.7 59.2 %copy-start.9 = (bf16[768,192]{0,1:T(8,128)(2,1)S(1)}, bf16[768,192]{0,1:T(8,128)(2,1)}, u32[]{:S(2)}) copy-start(bf16[768,192]{0,1:T(8,128)(2,1)} %param.36) | copy-start | bytes 884740
  601.7 185.8 %all-to-all-start.1 = ((bf16[16,2,73728]{2,1,0:T(2,128)(2,1)}), bf16[16,2,73728]{2,1,0:T(2,128)(2,1)}, u32[]{:S(2)}, u32[]{:S(2)}) async-start(bf16[16,2,73728]{2,1,0:T(2,128)(2,1)} %reshape.367), calls=%async_computation.9 | async-start | bytes 9437184 | tf_op jit(solution)/shard_map/all_to_all | solution.py:451
  659.5 66.3 %reduce-scatter.26.cloned.1.call-start = ((), (), s32[]{:S(2)}) async-start(), calls=%async_computation.18 | async-start | bytes 491520 | tf_op jit(solution)/shard_map/reduce_scatter | solution.py:104
  660.6 65.1 %copy-start.16 = (bf16[128,192]{0,1:T(8,128)(2,1)S(1)}, bf16[128,192]{0,1:T(8,128)(2,1)}, u32[]{:S(2)}) copy-start(bf16[128,192]{0,1:T(8,128)(2,1)} %param.30) | copy-start | bytes 147460
  660.6 65.1 %copy-start.36 = (f32[1,192]{1,0:T(1,128)S(1)}, f32[1,192]{1,0:T(1,128)}, u32[]{:S(2)}) copy-start(f32[1,192]{1,0:T(1,128)} %copy-done.35) | copy-start | bytes 2308
  660.7 65.1 %copy-start.46 = (f32[128]{0:T(128)S(1)}, f32[128]{0:T(128)}, u32[]{:S(2)}) copy-start(f32[128]{0:T(128)} %copy-done.45) | copy-start | bytes 1540
  660.7 65.1 %copy-start.48 = (f32[128]{0:T(128)S(1)}, f32[128]{0:T(128)}, u32[]{:S(2)}) copy-start(f32[128]{0:T(128)} %copy-done.47) | copy-start | bytes 1540
  660.7 88.4 %copy-start.13 = (f32[128,192]{0,1:T(8,128)S(1)}, f32[128,192]{0,1:T(8,128)}, u32[]{:S(2)}) copy-start(f32[128,192]{0,1:T(8,128)} %copy-done.12) | copy-start | bytes 294916
  660.7 88.4 %copy-start.17 = (f32[128,192]{0,1:T(8,128)S(1)}, f32[128,192]{0,1:T(8,128)}, u32[]{:S(2)}) copy-start(f32[128,192]{0,1:T(8,128)} %reduce-scatter.22.cloned.1.call-done) | copy-start | bytes 294916
  660.7 88.4 %copy-start.26 = (bf16[128,192]{0,1:T(8,128)(2,1)S(1)}, bf16[128,192]{0,1:T(8,128)(2,1)}, u32[]{:S(2)}) copy-start(bf16[128,192]{0,1:T(8,128)(2,1)} %param.31) | copy-start | bytes 147460
  660.7 88.4 %copy-start.33 = (f32[1,192]{1,0:T(1,128)S(1)}, f32[1,192]{1,0:T(1,128)}, u32[]{:S(2)}) copy-start(f32[1,192]{1,0:T(1,128)} %copy-done.32) | copy-start | bytes 2308
  660.7 88.4 %copy-start.42 = (f32[128]{0:T(128)S(1)}, f32[128]{0:T(128)}, u32[]{:S(2)}) copy-start(f32[128]{0:T(128)} %copy-done.41) | copy-start | bytes 1540
  660.7 88.4 %copy-start.44 = (f32[128]{0:T(128)S(1)}, f32[128]{0:T(128)}, u32[]{:S(2)}) copy-start(f32[128]{0:T(128)} %copy-done.43) | copy-start | bytes 1540
  660.7 88.4 %copy-start.51 = (f32[128]{0:T(128)S(1)}, f32[128]{0:T(128)}, u32[]{:S(2)}) copy-start(f32[128]{0:T(128)} %copy-done.50) | copy-start | bytes 1540
  660.7 88.4 %copy-start.53 = (f32[128]{0:T(128)S(1)}, f32[128]{0:T(128)}, u32[]{:S(2)}) copy-start(f32[128]{0:T(128)} %copy-done.52) | copy-start | bytes 1540
  660.8 88.4 %copy-start.57 = (f32[1,192]{1,0:T(1,128)S(1)}, f32[1,192]{1,0:T(1,128)}, u32[]{:S(2)}) copy-start(f32[1,192]{1,0:T(1,128)} %get-tuple-element.284) | copy-start | bytes 2308
  660.8 90.2 %copy-start.54 = (f32[192]{0:T(256)S(1)}, f32[192]{0:T(256)}, u32[]{:S(2)}) copy-start(f32[192]{0:T(256)} %get-tuple-element.222) | copy-start | bytes 2308
  660.8 90.2 %copy-start.55 = (f32[192]{0:T(256)S(1)}, f32[192]{0:T(256)}, u32[]{:S(2)}) copy-start(f32[192]{0:T(256)} %get-tuple-element.228) | copy-start | bytes 2308
  660.8 90.2 %copy-start.56 = (f32[192]{0:T(256)S(1)}, f32[192]{0:T(256)}, u32[]{:S(2)}) copy-start(f32[192]{0:T(256)} %get-tuple-element.268) | copy-start | bytes 2308
  660.8 126.0 %copy-start.34 = (f32[6,192]{1,0:T(8,128)S(1)}, f32[6,192]{1,0:T(8,128)}, u32[]{:S(2)}) copy-start(f32[6,192]{1,0:T(8,128)} %param.39) | copy-start | bytes 13828
  660.8 126.0 %copy-start.49 = (f32[6,192]{1,0:T(8,128)S(1)}, f32[6,192]{1,0:T(8,128)}, u32[]{:S(2)}) copy-start(f32[6,192]{1,0:T(8,128)} %param.46) | copy-start | bytes 13828
  660.9 88.3 %reduce-scatter.18.cloned.1.call-start = ((), (), s32[]{:S(2)}) async-start(), calls=%async_computation.14 | async-start | bytes 491520 | tf_op jit(solution)/shard_map/reduce_scatter | solution.py:104
  (23 other events, 134.6 us)
Sparse Core Ops, SparseCore 0:
  37.5 26.2 reduce-scatter.11
  84.6 20.9 reduce-scatter.13
  108.7 29.6 reduce-scatter.19
  141.2 31.0 reduce-scatter.15
  186.8 20.7 reduce-scatter.21
  234.5 21.3 reduce-scatter.23
  259.7 25.1 reduce-scatter.27
  299.2 19.0 all-reduce.10
  663.1 62.5 reduce-scatter.25
  728.5 20.5 reduce-scatter.17
where the time goes:
time: 840 us; the launch traced here: 831 us
  waiting for transfers between devices  328 us (39%)
  blocking collectives  182 us (22%)
  local copies, waits for them, and re-layouts  138 us (16%)
  starting transfers between devices  65.1 us (8%)
  other arithmetic  47 us (6%)
  matrix products  47 us (6%)
  between operations  15.2 us (2%)
  loops' own time  8.95 us (1%)
    all_to_all x1, waiting for transfers between devices, local(): lax.all_to_all(outgoing, ('row', 'col'), split_axis=0, concat_axis=0, til...  111 us
    reduce_scatter x4, waiting for transfers between devices, reduce_to_col(): lax.psum_scatter(term_rows(jnp.int32(0), own_rows * lax.axis_size('col'))...  100 us
    reduce_scatter x4, waiting for transfers between devices, reduce_to_row(): lax.psum_scatter(term_rows(jnp.int32(0), own_rows * lax.axis_size('row'))...  88.9 us
    all_to_all x1, starting transfers between devices, local(): lax.all_to_all(as_sent(outgoing_back), ('row', 'col'), split_axis=0, conc...  57.7 us
    unnamed x127, local copies, waits for them, and re-layouts  55.2 us
    all_gather x4, blocking collectives, tokens_over_col(): return lax.all_gather(local_piece, 'col', axis=0, tiled=True)  52.3 us
    all_gather x4, blocking collectives, tokens_over_row(): return lax.all_gather(local_piece, 'row', axis=0, tiled=True)  42.5 us
    psum x4, blocking collectives, feature_sums(): lax.psum((jnp.sum(first_term, axis=1, keepdims=True), jnp.sum(second_term...  38.9 us
  transfers between devices with their start and end apart: 12, of which 11 were waited for; matrix products, arithmetic and copies ran while one was open for 2% of the time, Pallas kernels for 0%

commit v1 on v0

v1 whole, which is shorter than its diff:
```python
import math

import jax
import jax.numpy as jnp
from jax import lax
from jax.sharding import PartitionSpec as P

HD = 64
NS_STEPS = 2


eps_norm = 1e-05
eps_gram = 1e-06
coef_a = 3.4445
coef_b = -4.775
coef_c = 2.0315
beta_mom = 0.95
rate_matrix = 0.03
rate_vector = 0.6


def gelu_value(values):
    return jax.nn.gelu(values, approximate=True)


def gelu_slope(values):
    return jax.vjp(gelu_value, values)[1](jnp.ones_like(values))[0]


def product(left_side, right_side, flip_right):
    if flip_right:
        return lax.dot_general(
            left_side, right_side, (((1,), (1,)), ((), ())), preferred_element_type=jnp.float32
        )
    return jnp.dot(left_side, right_side, preferred_element_type=jnp.float32)


def inner_rows(left_side, right_side):
    return lax.dot_general(
        left_side, right_side, (((0,), (0,)), ((), ())), preferred_element_type=jnp.float32
    )


def tile_grid(blocks, first_parts, second_parts):
    height = blocks.shape[1]
    breadth = blocks.shape[2]
    tiled = blocks.reshape(first_parts, second_parts, height, breadth)
    return tiled.transpose(0, 2, 1, 3).reshape(first_parts * height, second_parts * breadth)


def gather_grid(local_piece):
    blocks = lax.all_gather(local_piece, ("col", "row"), axis=0, tiled=False)
    return tile_grid(
        blocks.reshape((-1,) + local_piece.shape), lax.axis_size("col"), lax.axis_size("row")
    )


def norm_stats(values):
    mean_row = jnp.mean(values, axis=1, keepdims=True)
    square = jnp.mean(values * values, axis=1, keepdims=True)
    inv_std = lax.rsqrt(square - mean_row * mean_row + eps_norm)
    return mean_row, inv_std


def matrix_product(left_side, right_side):
    return jnp.dot(
        left_side.astype(jnp.bfloat16),
        right_side.astype(jnp.bfloat16),
        preferred_element_type=jnp.float32,
    )


def polynomial_factor(gram_matrix):
    gram_norm = jnp.sqrt(jnp.sum(gram_matrix * gram_matrix)) + eps_gram
    gram_now = gram_matrix / gram_norm
    poly_before = None
    for repeat in range(NS_STEPS):
        poly = coef_b * gram_now + coef_c * matrix_product(gram_now, gram_now)
        if poly_before is None:
            factor = poly
            scale = coef_a
        else:
            factor = coef_a * factor + scale * poly + matrix_product(poly, factor)
            scale = scale * coef_a
        if repeat + 1 < NS_STEPS:
            half = coef_a * gram_now + matrix_product(poly, gram_now)
            gram_now = coef_a * half + matrix_product(half, poly)
        poly_before = poly
    return factor, scale, gram_norm


def local(
    tokens,
    out_grad,
    segment_ids,
    w_qkv,
    w_out,
    w_fc,
    w_proj,
    bias_qkv,
    bias_fc,
    row_vectors,
    mom_qkv,
    mom_out,
    mom_fc,
    mom_proj,
    mom_bias_qkv,
    mom_bias_fc,
    mom_rows,
):
    low = jnp.bfloat16
    score_scale = 1.0 / math.sqrt(HD)
    row_parts = lax.axis_size("row")
    col_parts = lax.axis_size("col")
    dp_parts = lax.axis_size("dp")
    own_tokens, own_features = tokens.shape
    token_count = own_tokens * col_parts
    feature_count = own_features * row_parts
    token_base = lax.axis_index("col") * own_tokens
    feature_base = lax.axis_index("row") * own_features

    def own_columns(whole):
        return lax.dynamic_slice_in_dim(whole, feature_base, own_features, 1)

    def own_block(whole):
        return lax.dynamic_slice(whole, (token_base, feature_base), (own_tokens, own_features))

    def own_rows(whole):
        return lax.dynamic_slice_in_dim(whole, token_base, own_tokens, 0)

    tokens_all = gather_grid(tokens)
    qkv_cols = lax.all_gather(w_qkv, "row", axis=0, tiled=True)
    vectors_all = lax.all_gather(row_vectors, "row", axis=1, tiled=True)
    out_whole = gather_grid(w_out)
    fc_cols = lax.all_gather(w_fc, "row", axis=0, tiled=True)
    grad_all = gather_grid(out_grad)
    proj_flip = w_proj.T
    proj_cols = lax.all_gather(proj_flip, "row", axis=0, tiled=True)
    gain_one, shift_one, gain_two, shift_two, bias_out, _ = [
        vectors_all[which] for which in range(6)
    ]

    resid_in = tokens_all.astype(jnp.float32)
    mean_one, inv_one = norm_stats(resid_in)
    unit_one = (resid_in - mean_one) * inv_one
    act_one = (unit_one * gain_one + shift_one).astype(low)
    qkv_local = (product(act_one, qkv_cols, False) + bias_qkv).astype(low)
    heads_local = qkv_local.shape[1] // (3 * HD)
    qkv_tiles = qkv_local.reshape(token_count, heads_local, 3, HD).transpose(2, 1, 0, 3)
    query, key, value = qkv_tiles[0], qkv_tiles[1], qkv_tiles[2]
    segment_row = segment_ids[0]
    positions = jnp.arange(token_count, dtype=jnp.int32)
    allowed = (positions[None, :] <= positions[:, None]) & (
        segment_row[None, :] == segment_row[:, None]
    )
    scores = (
        jnp.einsum("hqe,hke->hqk", query, key, preferred_element_type=jnp.float32) * score_scale
    )
    scores = jnp.where(allowed[None], scores, -jnp.inf)
    row_max = jnp.max(scores, axis=2, keepdims=True)
    raised = jnp.exp(scores - row_max)
    probs = raised / jnp.sum(raised, axis=2, keepdims=True)
    prob_low = probs.astype(low)
    attended = jnp.einsum(
        "hqk,hke->hqe", prob_low, value, preferred_element_type=jnp.float32
    ).astype(low)
    attn_local = attended.transpose(1, 0, 2).reshape(token_count, heads_local * HD)
    attn_all = lax.all_gather(attn_local, "col", axis=1, tiled=True)
    resid_mid = resid_in + product(attn_all, out_whole, False) + bias_out
    mean_two, inv_two = norm_stats(resid_mid)
    unit_two = (resid_mid - mean_two) * inv_two
    act_two = (unit_two * gain_two + shift_two).astype(low)
    hidden_pre = product(act_two, fc_cols, False) + bias_fc
    hidden = gelu_value(hidden_pre).astype(low)
    grad_hidden = product(grad_all, proj_cols, False)
    grad_pre = (gelu_slope(hidden_pre) * grad_hidden).astype(low)

    grad_norm_two = lax.psum_scatter(
        product(grad_pre, w_fc, True).astype(low), "col", scatter_dimension=0, tiled=True
    )
    grad_two_all = gather_grid(grad_norm_two).astype(jnp.float32)
    grad_norm_two = grad_norm_two.astype(jnp.float32)
    scaled = grad_two_all * gain_two
    first_mean = jnp.mean(scaled, axis=1, keepdims=True)
    second_mean = jnp.mean(scaled * unit_two, axis=1, keepdims=True)
    grad_mid_all = grad_all.astype(jnp.float32) + inv_two * (
        scaled - first_mean - unit_two * second_mean
    )
    grad_mid_low = grad_mid_all.astype(low)
    out_rows = lax.dynamic_slice_in_dim(
        out_whole, lax.axis_index("col") * w_out.shape[0], w_out.shape[0], 0
    )
    grad_attn = (
        product(grad_mid_low, out_rows, True)
        .astype(low)
        .reshape(token_count, heads_local, HD)
        .transpose(1, 0, 2)
    )

    grad_value = jnp.einsum(
        "hqk,hqe->hke", prob_low, grad_attn, preferred_element_type=jnp.float32
    )
    grad_probs = jnp.einsum("hqe,hke->hqk", grad_attn, value, preferred_element_type=jnp.float32)
    row_dot = jnp.sum(
        grad_attn.astype(jnp.float32) * attended.astype(jnp.float32), axis=2, keepdims=True
    )
    grad_scores = (score_scale * probs * (grad_probs - row_dot)).astype(low)
    grad_query = jnp.einsum("hqk,hke->hqe", grad_scores, key, preferred_element_type=jnp.float32)
    grad_key = jnp.einsum("hqk,hqe->hke", grad_scores, query, preferred_element_type=jnp.float32)
    grad_qkv_low = (
        jnp.stack([grad_query.astype(low), grad_key.astype(low), grad_value.astype(low)], axis=0)
        .transpose(2, 1, 0, 3)
        .reshape(token_count, heads_local * 3 * HD)
    )

    grad_blocks = (
        inner_rows(own_columns(act_one), grad_qkv_low),
        inner_rows(attn_local, own_columns(grad_mid_low)),
        inner_rows(own_columns(act_two), grad_pre),
        inner_rows(hidden, own_columns(grad_all)),
    )
    summed = [lax.psum(block.astype(low), "dp").astype(jnp.float32) for block in grad_blocks]
    bias_sums = lax.psum(
        (
            jnp.sum(grad_qkv_low, axis=0, dtype=jnp.float32),
            jnp.sum(grad_pre, axis=0, dtype=jnp.float32),
        ),
        "dp",
    )
    summed = summed + list(bias_sums)

    weights = (w_qkv, w_out, w_fc, w_proj)
    moments = (mom_qkv, mom_out, mom_fc, mom_proj)
    flips = (False, True, False, True)
    new_moms = [beta_mom * moments[member] + summed[member] for member in range(4)]
    pushes = [
        (summed[member] + beta_mom * new_moms[member]).astype(low) for member in range(4)
    ]
    upright = [pushes[member].T if flips[member] else pushes[member] for member in range(4)]
    widest = max(piece.shape[1] for piece in upright)
    share = -(-widest // dp_parts)
    assert row_parts == len(upright)
    outgoing = jnp.stack(
        [
            jnp.pad(piece, ((0, 0), (0, share * dp_parts - piece.shape[1])))
            for piece in upright
        ]
    )
    outgoing = lax.dynamic_slice_in_dim(outgoing, lax.axis_index("dp") * share, share, 2)
    arrived = lax.all_to_all(outgoing, "row", split_axis=0, concat_axis=0, tiled=True)
    matrix = arrived.reshape(feature_count, share)
    gram = lax.psum(product(matrix, matrix, True).astype(low), ("dp", "col")).astype(jnp.float32)
    factor, scale, gram_norm = polynomial_factor(gram)
    ortho = (scale * matrix.astype(jnp.float32) + matrix_product(factor, matrix)) * lax.rsqrt(
        gram_norm
    )
    back = lax.all_to_all(
        ortho.astype(low).reshape(row_parts, own_features, share),
        "row",
        split_axis=0,
        concat_axis=0,
        tiled=True,
    )
    orthos = lax.all_gather(back, "dp", axis=2, tiled=True)
    new_weights = []
    for member in range(4):
        piece = orthos[member, :, : upright[member].shape[1]]
        if flips[member]:
            piece = piece.T
        longest = max(
            upright[member].shape[0] * row_parts, upright[member].shape[1] * col_parts
        )
        new_weights.append(
            weights[member].astype(jnp.float32)
            - rate_matrix * math.sqrt(longest) * piece.astype(jnp.float32)
        )

    block_sum = lax.psum_scatter(
        product(hidden, proj_flip, True).astype(low), "col", scatter_dimension=0, tiled=True
    ).astype(jnp.float32)
    block_out = (own_block(resid_mid) + block_sum + row_vectors[5]).astype(low)
    grad_norm_one = lax.psum_scatter(
        product(grad_qkv_low, w_qkv, True).astype(low), "col", scatter_dimension=0, tiled=True
    ).astype(jnp.float32)
    unit_one_own = own_block(unit_one)
    scaled_one = grad_norm_one * row_vectors[0]
    first_sum, second_sum = lax.psum(
        (
            jnp.sum(scaled_one, axis=1, keepdims=True),
            jnp.sum(scaled_one * unit_one_own, axis=1, keepdims=True),
        ),
        "row",
    )
    input_grad = own_block(grad_mid_all) + own_rows(inv_one) * (
        scaled_one - first_sum / feature_count - unit_one_own * (second_sum / feature_count)
    )
    row_terms = jnp.stack(
        [
            jnp.sum(grad_norm_one * unit_one_own, axis=0),
            jnp.sum(grad_norm_one, axis=0),
            jnp.sum(grad_norm_two * own_block(unit_two), axis=0),
            jnp.sum(grad_norm_two, axis=0),
            jnp.sum(own_block(grad_mid_low), axis=0, dtype=jnp.float32),
            jnp.sum(out_grad, axis=0, dtype=jnp.float32),
        ]
    )
    grad_rows = lax.psum(row_terms, ("dp", "col"))
    vector_rate = rate_vector / math.sqrt(token_count * dp_parts)

    def vector_step(weight, gradient, moment):
        new_moment = beta_mom * moment + gradient
        return (weight - vector_rate * (gradient + beta_mom * new_moment), new_moment)

    new_bias_qkv, new_mom_bias_qkv = vector_step(bias_qkv, summed[4], mom_bias_qkv)
    new_bias_fc, new_mom_bias_fc = vector_step(bias_fc, summed[5], mom_bias_fc)
    new_rows, new_mom_rows = vector_step(row_vectors, grad_rows, mom_rows)
    return (
        block_out,
        input_grad,
        summed[0],
        summed[1],
        summed[2],
        summed[3],
        summed[4],
        summed[5],
        grad_rows,
        new_weights[0],
        new_weights[1],
        new_weights[2],
        new_weights[3],
        new_bias_qkv,
        new_bias_fc,
        new_rows,
        new_moms[0],
        new_moms[1],
        new_moms[2],
        new_moms[3],
        new_mom_bias_qkv,
        new_mom_bias_fc,
        new_mom_rows,
    )


def solution(mesh):
    placed = (
        P(("dp", "col"), "row"),
        P(("dp", "col"), "row"),
        P("dp", None),
        P("row", "col"),
        P("col", "row"),
        P("row", "col"),
        P("col", "row"),
        P("col"),
        P("col"),
        P(None, "row"),
        P("row", "col"),
        P("col", "row"),
        P("row", "col"),
        P("col", "row"),
        P("col"),
        P("col"),
        P(None, "row"),
    )
    return jax.shard_map(
        local,
        mesh=mesh,
        in_specs=placed,
        out_specs=(
            P(("dp", "col"), "row"),
            P(("dp", "col"), "row"),
            P("row", "col"),
            P("col", "row"),
            P("row", "col"),
            P("col", "row"),
            P("col"),
            P("col"),
            P(None, "row"),
            P("row", "col"),
            P("col", "row"),
            P("row", "col"),
            P("col", "row"),
            P("col"),
            P("col"),
            P(None, "row"),
            P("row", "col"),
            P("col", "row"),
            P("row", "col"),
            P("col", "row"),
            P("col"),
            P("col"),
            P(None, "row"),
        ),
        check_vma=False,
    )
```

time: 840 us -> 444 us (0.53)
  waiting for transfers between devices: 328 us -> 92.2 us
  local copies, waits for them, and re-layouts: 138 us -> 36.4 us
  starting transfers between devices: 65.1 us -> 4.38 us
  blocking collectives: 182 us -> 213 us
  other arithmetic: 47 us -> 32 us
  loops' own time: 8.95 us -> 0 us
    reduce_scatter x8 -> x3, waiting for transfers between devices: 189 us -> 23.3 us  [the longest x1 12.3 us: local(): lax.psum_scatter(product(grad_pre, w_fc, True).astype(low), 'col', scatte...]
    all_to_all x2 -> x1, waiting for transfers between devices: 111 us -> 0.51 us  [local(): lax.all_to_all(ortho.astype(low).reshape(row_parts, own_features, share),...]
    all_gather x9 -> x6, blocking collectives: 104 us -> 173 us  [the longest x3 136 us: gather_grid(): blocks = lax.all_gather(local_piece, ('col', 'row'), axis=0, tiled=False)]
    all_to_all x2 -> x1, starting transfers between devices: 64.6 us -> 3.77 us  [local(): lax.all_to_all(ortho.astype(low).reshape(row_parts, own_features, share),...]
    psum x1 -> x2, waiting for transfers between devices: 19.2 us -> 66.2 us  [the longest x1 50.5 us: local(): lax.psum(product(matrix, matrix, True).astype(low), ('dp', 'col'))]
    unnamed x127 -> x105, local copies, waits for them, and re-layouts: 55.2 us -> 16.8 us
    psum x5 -> x2, blocking collectives: 41.4 us -> 12.4 us  [the longest x1 9.86 us: local(): lax.psum((jnp.sum(scaled_one, axis=1, keepdims=True), jnp.sum(scaled_one...]
    scatter x4 -> x0, local copies, waits for them, and re-layouts: 27.4 us -> none  [local(): outgoing.at[owner_slots[member], :sizes_flat[member]]]
  transfers between devices with their start and end apart: 12 -> 10, of which waited for: 11 -> 5; matrix products, arithmetic and copies ran while one was open for 2% -> 17% of each run, Pallas kernels for 0% -> 0%
where the time goes in v1:
time: 444 us; the launch traced here: 443 us
  blocking collectives  213 us (48%)
  waiting for transfers between devices  92.2 us (21%)
  matrix products  49.5 us (11%)
  local copies, waits for them, and re-layouts  36.4 us (8%)
  other arithmetic  32 us (7%)
  between operations  15.2 us (3%)
    all_gather x3, blocking collectives, gather_grid(): blocks = lax.all_gather(local_piece, ('col', 'row'), axis=0, tiled=False)  136 us
    psum x1, waiting for transfers between devices, local(): lax.psum(product(matrix, matrix, True).astype(low), ('dp', 'col'))  50.5 us
    unnamed x105, local copies, waits for them, and re-layouts  16.8 us
    all_gather x1, blocking collectives, local(): attn_all = lax.all_gather(attn_local, 'col', axis=1, tiled=True)  16.6 us
    psum x1, waiting for transfers between devices, local(): lax.psum(block.astype(low), 'dp').astype(jnp.float32)  15.7 us
    dot_general x5, matrix products, matrix_product(): jnp.dot(left_side.astype(jnp.bfloat16), right_side.astype(jnp.bfloat16),...  14.5 us
    psum x1, blocking collectives, local(): grad_rows = lax.psum(row_terms, ('dp', 'col'))  14.4 us
    all_to_all x1, blocking collectives, local(): lax.all_to_all(outgoing, 'row', split_axis=0, concat_axis=0, tiled=True)  13.6 us
  transfers between devices with their start and end apart: 10, of which 5 were waited for; matrix products, arithmetic and copies ran while one was open for 17% of the time, Pallas kernels for 0%

profile of v1, /device:TPU:0, one launch (start us, length us, event | category | flops | bytes accessed | tf_op | source)
XLA Modules:
  0.0 442.9 jit_solution(18156364736476720442)
XLA Ops:
  9.5 47.6 %all-gather = bf16[2048,192]{0,1:T(8,128)(2,1)S(1)} all-gather(bf16[128,192]{0,1:T(8,128)(2,1)} %param.17), channel_id=2, replica_groups=mesh['dp'=2,'row'=4,'col'=4] {'col','row'}, dimensions={0}, use_global_device_ids=true | all-gather | bytes 835584 | tf_op jit(solution)/shard_map/all_gather | solution.py:52
  57.0 1.3 reshape.265
  60.2 6.9 %all-gather.4 = f32[4,192,6]{1,2,0:T(8,128)S(1)} all-gather(f32[1,192,6]{1,2,0:T(8,128)S(1)} %bitcast.210), channel_id=1, replica_groups=mesh['dp'=2,'row'=4,'col'=4] {'row'}, dimensions={0}, use_global_device_ids=true | all-gather | bytes 23040 | tf_op jit(solution)/shard_map/all_gather | solution.py:133
  69.0 13.3 %all_gather.45 = bf16[768,576]{1,0:T(8,128)(2,1)S(1)} all-gather(bf16[192,576]{1,0:T(8,128)(2,1)S(1)} %copy-done.16), channel_id=1, replica_groups=mesh['dp'=2,'row'=4,'col'=4] {'row'}, dimensions={0}, use_global_device_ids=true | all-gather | bytes 1105920 | tf_op jit(solution)/shard_map/all_gather | solution.py:132
  82.2 1.5 add_convert_fusion.1
  85.5 43.6 %all-gather.2 = bf16[2048,192]{0,1:T(8,128)(2,1)S(1)} all-gather(bf16[128,192]{0,1:T(8,128)(2,1)S(1)} %copy-done.30), channel_id=4, replica_groups=mesh['dp'=2,'row'=4,'col'=4] {'col','row'}, dimensions={0}, use_global_device_ids=true | all-gather | bytes 835584 | tf_op jit(solution)/shard_map/all_gather | solution.py:52
  131.5 4.1 fusion.73
  135.6 2.3 fusion.19
  137.9 1.5 convolution_convert_fusion.6
  139.4 16.6 %all_gather.46 = bf16[512,768]{0,1:T(8,128)(2,1)} all-gather(bf16[512,192]{0,1:T(8,128)(2,1)S(1)} %bitcast.195), channel_id=1, replica_groups=mesh['dp'=2,'row'=4,'col'=4] {'col'}, dimensions={1}, use_global_device_ids=true | all-gather | bytes 983040 | tf_op jit(solution)/shard_map/all_gather | solution.py:168
  156.0 3.9 copy.219
  159.9 3.1 reshape.253
  163.0 2.6 fusion.70
  168.0 3.8 multiply_convert_fusion.1
  171.9 4.2 convert_reduce_fusion
  178.4 2.5 convolution_convert_fusion.2
  180.8 2.0 convolution_convert_fusion.1
  182.8 12.3 %reduce-scatter.12.cloned.1.call-done = bf16[128,192]{1,0:T(8,128)(2,1)} async-done(((bf16[512,192]{1,0:T(8,128)(2,1)}), bf16[128,192]{1,0:T(8,128)(2,1)}) %reduce-scatter.12.cloned.1.call-update) | async-done | bytes 49168 | tf_op jit(solution)/shard_map/reduce_scatter | solution.py:178
  196.0 44.7 %all-gather.3 = bf16[2048,192]{0,1:T(8,128)(2,1)} all-gather(bf16[128,192]{0,1:T(8,128)(2,1)S(1)} %copy.201), channel_id=5, replica_groups=mesh['dp'=2,'row'=4,'col'=4] {'col','row'}, dimensions={0}, use_global_device_ids=true | all-gather | bytes 835584 | tf_op jit(solution)/shard_map/all_gather | solution.py:52
  240.7 2.3 reshape.266
  243.4 1.3 copy.217
  244.7 3.1 copy.174
  247.8 1.7 multiply_reduce_fusion
  251.0 1.7 fusion.71
  252.7 1.5 convolution_convert_fusion.9
  257.9 2.3 convolution_convert_fusion.3
  260.4 15.7 %all-reduce.10.cloned.1.call-done = (bf16[192,192]{0,1:T(8,128)(2,1)}, bf16[192,576]{1,0:T(8,128)(2,1)}, bf16[192,768]{1,0:T(8,128)(2,1)}, bf16[768,192]{0,1:T(8,128)(2,1)}) async-done(((bf16[192,192]{0,1:T(8,128)(2,1)}, bf16[192,576]{1,0:T(8,128)(2,1)}, bf16[192,768]{1,0:T(8,128)(2,1)}, bf16[768,192]{0,1:T(8,128)(2,1)}), (bf16[192,192]{0,1:T(8,128)(2,1)}, bf16[192,576]{1,0:T(8,128)(2,1)}, ...) | async-done | bytes 884752 | tf_op jit(solution)/shard_map/psum | solution.py:222
  276.1 2.2 add_convert_fusion.4
  281.7 13.6 %all_to_all.10 = bf16[4,192,384]{2,1,0:T(8,128)(2,1)S(1)} all-to-all(bf16[4,192,384]{2,1,0:T(8,128)(2,1)S(1)} %fusion.34), channel_id=1, replica_groups=mesh['dp'=2,'row'=4,'col'=4] {'row'}, dimensions={0} | all-to-all | bytes 1179648 | tf_op jit(solution)/shard_map/all_to_all | solution.py:250
  295.3 1.8 convolution_convert_fusion
  297.2 2.3 convolution_convert_fusion.11
  299.5 1.8 copy.198
  302.1 1.9 convolution_convert_fusion.4
  304.1 1.8 copy.202
  305.9 50.5 %all-reduce.8.cloned.1.call-done = bf16[768,768]{1,0:T(8,128)(2,1)} async-done(((bf16[768,768]{1,0:T(8,128)(2,1)}), bf16[768,768]{1,0:T(8,128)(2,1)}) %all-reduce.8.cloned.1.call-update) | async-done | bytes 1179664 | tf_op jit(solution)/shard_map/psum | solution.py:252
  356.4 2.5 fusion.2
  359.6 3.4 multiply_add_fusion.4
  365.6 2.5 multiply_add_fusion.1
  368.1 6.3 %fusion.18 = bf16[768,384]{1,0:T(8,128)(2,1)} fusion(bf16[768,384]{1,0:T(8,128)(2,1)S(1)} %bitcast.188, f32[768,768]{1,0:T(8,128)} %copy-done.13, f32[768,768]{1,0:T(8,128)} %multiply_add_fusion.1, f32[]{:T(128)S(6)} %rsqrt.28), kind=kOutput, calls=%fused_computation.51 | convolution fusion | flops 1363968000 | bytes 5898244 | tf_op jit(solution)/shard_map/dot_general | solution.py:66
  374.5 3.8 all-to-all-start.1
  381.0 2.6 all-reduce.3
  388.3 11.0 %reduce-scatter.14.cloned.1.call-done = bf16[128,192]{1,0:T(8,128)(2,1)} async-done(((bf16[512,192]{1,0:T(8,128)(2,1)}), bf16[128,192]{1,0:T(8,128)(2,1)}) %reduce-scatter.14.cloned.1.call-update) | async-done | bytes 49168 | tf_op jit(solution)/shard_map/reduce_scatter | solution.py:282
  400.5 9.9 %all-reduce.2 = (f32[128,1]{0,1:T(1,128)S(1)}, f32[128,1]{0,1:T(1,128)S(1)}) all-reduce(f32[128,1]{0,1:T(1,128)S(1)} %bitcast.222, f32[128,1]{0,1:T(1,128)S(1)} %bitcast.223), channel_id=1, replica_groups=mesh['dp'=2,'row'=4,'col'=4] {'row'}, use_global_device_ids=true, to_apply=%region_15.16 | all-reduce | flops 256 | bytes 2048 | tf_op jit(solution)/shard_map/psum | solution.py:287
  410.4 1.3 fusion.51
  412.4 14.4 %psum.78 = f32[6,192]{1,0:T(8,128)S(1)} all-reduce(f32[6,192]{1,0:T(8,128)S(1)} %stack.58), channel_id=1, replica_groups=mesh['dp'=2,'row'=4,'col'=4] {'dp','col'}, use_global_device_ids=true, to_apply=%region_30.31 | all-reduce | flops 1152 | bytes 9216 | tf_op jit(solution)/shard_map/psum | solution.py:307
  430.8 1.8 bitcast_subtract_fusion.2
  432.6 1.9 bitcast_subtract_fusion.1
  434.5 1.9 bitcast_subtract_fusion
  (178 shorter events, 41.2 us)
Async XLA Ops:
  7.2 148.8 %all-gather.16.cloned.1.call-start = ((), (), s32[]{:S(2)}) async-start(), calls=%async_computation.9 | async-start | bytes 1671168 | tf_op jit(solution)/shard_map/all_gather | solution.py:52
  7.9 160.1 %all-gather.10.cloned.1.call-start = ((), (), s32[]{:S(2)}) async-start(), calls=%async_computation.5 | async-start | bytes 1474560 | tf_op jit(solution)/shard_map/all_gather | solution.py:135
  8.7 163.2 %all-gather.12.cloned.1.call-start = ((), (), s32[]{:S(2)}) async-start(), calls=%async_computation.6 | async-start | bytes 1474560 | tf_op jit(solution)/shard_map/all_gather | solution.py:138
  9.4 185.6 %reduce-scatter.12.cloned.1.call-start = ((), (), s32[]{:S(2)}) async-start(), calls=%async_computation.11 | async-start | bytes 327680 | tf_op jit(solution)/shard_map/reduce_scatter | solution.py:178
  58.7 1.4 copy-start.32
  67.4 1.6 copy-start.16
  82.2 1.5 copy-start.37
  83.7 1.7 copy-start.30
  130.0 1.5 copy-start.6
  130.3 5.2 %copy-start.3 = (bf16[96,8,4,128]{3,1,2,0:T(8,128)(2,1)}, bf16[96,8,4,128]{3,1,2,0:T(8,128)(2,1)S(1)}, u32[]{:S(2)}) copy-start(bf16[96,8,4,128]{3,1,2,0:T(8,128)(2,1)S(1)} %copy.220) | copy-start | bytes 2359300
  137.9 22.0 %copy-start.1 = (bf16[3,512,512]{1,2,0:T(8,128)(2,1)}, bf16[3,512,512]{1,2,0:T(8,128)(2,1)S(1)}, u32[]{:S(2)}) copy-start(bf16[3,512,512]{1,2,0:T(8,128)(2,1)S(1)} %fusion.19) | copy-start | bytes 4718596
  163.0 2.6 copy-start.19
  168.0 3.8 copy-start.7
  171.9 9.0 %copy-start.5 = (bf16[512,768]{1,0:T(8,128)(2,1)}, bf16[512,768]{1,0:T(8,128)(2,1)S(1)}, u32[]{:S(2)}) copy-start(bf16[512,768]{1,0:T(8,128)(2,1)S(1)} %get-tuple-element.218) | copy-start | bytes 2359300
  171.9 5.2 %copy-start.10 = (bf16[192,768]{1,0:T(8,128)(2,1)S(1)}, bf16[192,768]{1,0:T(8,128)(2,1)}, u32[]{:S(2)}) copy-start(bf16[192,768]{1,0:T(8,128)(2,1)} %param.22) | copy-start | bytes 884740
  178.3 97.8 %all-reduce.10.cloned.1.call-start = ((), (), s32[]{:S(2)}) async-start(), calls=%async_computation.13 | async-start | bytes 1867776 | tf_op jit(solution)/shard_map/psum | solution.py:222
  247.8 2.1 copy-start.9
  249.5 1.4 copy-start
  250.9 3.2 copy-start.2
  251.0 3.9 copy-start.15
  252.7 2.2 copy-start.4
  257.8 2.4 copy-start.31
  260.2 96.2 %all-reduce.8.cloned.1.call-start = ((), (), s32[]{:S(2)}) async-start(), calls=%async_computation.7 | async-start | bytes 2359296 | tf_op jit(solution)/shard_map/psum | solution.py:252
  276.1 2.2 copy-start.23
  276.1 2.2 copy-start.28
  278.3 1.4 copy-start.27
  279.4 1.4 copy-start.25
  297.1 86.5 %reduce-scatter.10.cloned.1.call-start = ((), (), s32[]{:S(2)}) async-start(), calls=%async_computation.10 | async-start | bytes 327680 | tf_op jit(solution)/shard_map/reduce_scatter | solution.py:278
  301.2 98.1 %reduce-scatter.14.cloned.1.call-start = ((), (), s32[]{:S(2)}) async-start(), calls=%async_computation.12 | async-start | bytes 327680 | tf_op jit(solution)/shard_map/reduce_scatter | solution.py:282
  359.6 3.4 copy-start.21
  363.0 1.4 copy-start.13
  374.4 11.7 %copy-start.38 = (f32[576]{0:T(1024)S(1)}, f32[576]{0:T(1024)}, u32[]{:S(2)}) copy-start(f32[576]{0:T(1024)} %param.24) | copy-start | bytes 6916
  374.4 11.7 %copy-start.39 = (f32[576]{0:T(1024)S(1)}, f32[576]{0:T(1024)}, u32[]{:S(2)}) copy-start(f32[576]{0:T(1024)} %param.31) | copy-start | bytes 6916
  374.4 13.1 %copy-start.29 = (bf16[128,192]{1,0:T(8,128)(2,1)S(1)}, bf16[128,192]{1,0:T(8,128)(2,1)}, u32[]{:S(2)}) copy-start(bf16[128,192]{1,0:T(8,128)(2,1)} %reduce-scatter.12.cloned.1.call-done) | copy-start | bytes 147460
  374.4 13.3 %copy-start.41 = (f32[768]{0:T(1024)S(1)}, f32[768]{0:T(1024)}, u32[]{:S(2)}) copy-start(f32[768]{0:T(1024)} %param.25) | copy-start | bytes 9220
  374.4 13.3 %copy-start.42 = (f32[768]{0:T(1024)S(1)}, f32[768]{0:T(1024)}, u32[]{:S(2)}) copy-start(f32[768]{0:T(1024)} %param.32) | copy-start | bytes 9220
  374.5 24.9 %copy-start.34 = (f32[1,192]{1,0:T(1,128)S(1)}, f32[1,192]{1,0:T(1,128)}, u32[]{:S(2)}) copy-start(f32[1,192]{1,0:T(1,128)} %get-tuple-element.209) | copy-start | bytes 2308
  374.5 52.4 %copy-start.36 = (f32[6,192]{1,0:T(8,128)S(1)}, f32[6,192]{1,0:T(8,128)}, u32[]{:S(2)}) copy-start(f32[6,192]{1,0:T(8,128)} %param.33) | copy-start | bytes 13828
  374.5 10.8 %all-to-all-start.1 = ((bf16[4,192,384]{2,1,0:T(8,128)(2,1)}), bf16[4,192,384]{2,1,0:T(8,128)(2,1)S(1)}, u32[]{:S(2)}, u32[]{:S(2)}) async-start(bf16[4,192,384]{2,1,0:T(8,128)(2,1)} %bitcast.207), calls=%async_computation.1 | async-start | bytes 1179648 | tf_op jit(solution)/shard_map/all_to_all | solution.py:257
  378.2 49.2 %copy-start.26 = (bf16[192,192]{0,1:T(8,128)(2,1)S(1)}, bf16[192,192]{0,1:T(8,128)(2,1)}, u32[]{:S(2)}) copy-start(bf16[192,192]{0,1:T(8,128)(2,1)} %get-tuple-element.180) | copy-start | bytes 221188
  378.3 50.0 %copy-start.22 = (f32[192,192]{0,1:T(8,128)S(1)}, f32[192,192]{0,1:T(8,128)}, u32[]{:S(2)}) copy-start(f32[192,192]{0,1:T(8,128)} %get-tuple-element.207) | copy-start | bytes 442372
  378.3 50.8 %all-gather.14.cloned.1.call-start = ((), (), s32[]{:S(2)}) async-start(), calls=%async_computation.8 | async-start | bytes 1769472 | tf_op jit(solution)/shard_map/all_gather | solution.py:264
  383.6 46.4 %copy-start.43 = (f32[576]{0:T(1024)}, f32[576]{0:T(1024)S(1)}, u32[]{:S(2)}) copy-start(f32[576]{0:T(1024)S(1)} %get-tuple-element.178) | copy-start | bytes 6916
  383.6 46.4 %copy-start.44 = (f32[768]{0:T(1024)}, f32[768]{0:T(1024)S(1)}, u32[]{:S(2)}) copy-start(f32[768]{0:T(1024)S(1)} %get-tuple-element.179) | copy-start | bytes 9220
  386.1 44.7 %copy-start.17 = (bf16[192,576]{1,0:T(8,128)(2,1)S(1)}, bf16[192,576]{1,0:T(8,128)(2,1)}, u32[]{:S(2)}) copy-start(bf16[192,576]{1,0:T(8,128)(2,1)} %param.20) | copy-start | bytes 663556
  410.4 22.2 %copy-start.11 = (bf16[192,768]{1,0:T(8,128)(2,1)S(1)}, bf16[192,768]{1,0:T(8,128)(2,1)}, u32[]{:S(2)}) copy-start(bf16[192,768]{1,0:T(8,128)(2,1)} %param.22) | copy-start | bytes 884740
  426.9 7.6 %copy-start.33 = (f32[6,192]{1,0:T(8,128)}, f32[6,192]{1,0:T(8,128)S(1)}, u32[]{:S(2)}) copy-start(f32[6,192]{1,0:T(8,128)S(1)} %psum.78) | copy-start | bytes 13828
  428.3 6.2 %copy-start.12 = (bf16[768,192]{0,1:T(8,128)(2,1)S(1)}, bf16[768,192]{0,1:T(8,128)(2,1)}, u32[]{:S(2)}) copy-start(bf16[768,192]{0,1:T(8,128)(2,1)} %param.23) | copy-start | bytes 884740
  (7 other events, 6.8 us)
Sparse Core Ops, SparseCore 0:
  10.8 64.3 all-gather.15
  77.0 32.6 all-gather.9
  111.6 27.0 all-gather.11
  178.4 16.5 reduce-scatter.11
  260.3 15.7 all-reduce.9
  297.2 59.0 all-reduce.7
  359.2 19.0 reduce-scatter.9
  381.1 18.2 reduce-scatter.13
  401.5 7.4 all-gather.13

commit v2 on v1

--- a/solution.py
+++ b/solution.py
@@ -1,8 +1,11 @@
+import functools
 import math
 
 import jax
 import jax.numpy as jnp
 from jax import lax
+from jax.experimental import pallas as pl
+from jax.experimental.pallas import tpu as pltpu
 from jax.sharding import PartitionSpec as P
 
 HD = 64
@@ -41,18 +44,83 @@
     )
 
 
-def tile_grid(blocks, first_parts, second_parts):
-    height = blocks.shape[1]
-    breadth = blocks.shape[2]
-    tiled = blocks.reshape(first_parts, second_parts, height, breadth)
-    return tiled.transpose(0, 2, 1, 3).reshape(first_parts * height, second_parts * breadth)
-
-
-def gather_grid(local_piece):
-    blocks = lax.all_gather(local_piece, ("col", "row"), axis=0, tiled=False)
-    return tile_grid(
-        blocks.reshape((-1,) + local_piece.shape), lax.axis_size("col"), lax.axis_size("row")
-    )
+def exchange_kernel(axis, parts, kinds, *refs):
+    count = len(kinds)
+    sources, targets = refs[:count], refs[count : 2 * count]
+    send_sem, recv_sem, local_sem = refs[2 * count :]
+    me = lax.axis_index(axis)
+    barrier = pltpu.get_barrier_semaphore()
+    for step in range(1, parts):
+        peer = lax.rem(me + step, parts)
+        pl.semaphore_signal(
+            barrier, inc=1, device_id={axis: peer}, device_id_type=pl.DeviceIdType.MESH
+        )
+    pl.semaphore_wait(barrier, parts - 1)
+    copies = []
+    for which in range(count):
+        for step in range(1, parts):
+            peer = lax.rem(me + step, parts)
+            copy = pltpu.make_async_remote_copy(
+                src_ref=sources[which].at[peer] if kinds[which] else sources[which],
+                dst_ref=targets[which].at[me],
+                send_sem=send_sem.at[which, step - 1],
+                recv_sem=recv_sem.at[which, step - 1],
+                device_id={axis: peer},
+                device_id_type=pl.DeviceIdType.MESH,
+            )
+            copy.start()
+            copies.append(copy)
+    for which in range(count):
+        copy = pltpu.make_async_copy(
+            sources[which].at[me] if kinds[which] else sources[which],
+            targets[which].at[me],
+            local_sem.at[which],
+        )
+        copy.start()
+        copies.append(copy)
+    for copy in copies:
+        copy.wait()
+
+
+def exchange(axis, arrays, kinds, name_id):
+    parts = lax.axis_size(axis)
+    count = len(arrays)
+    shapes = [
+        jax.ShapeDtypeStruct(
+            array.shape if kind else (parts,) + array.shape, array.dtype
+        )
+        for array, kind in zip(arrays, kinds)
+    ]
+    return pl.pallas_call(
+        functools.partial(exchange_kernel, axis, parts, tuple(kinds)),
+        out_shape=shapes,
+        in_specs=[pl.BlockSpec(memory_space=pltpu.VMEM)] * count,
+        out_specs=[pl.BlockSpec(memory_space=pltpu.VMEM)] * count,
+        scratch_shapes=[
+            pltpu.SemaphoreType.DMA((count, parts - 1)),
+            pltpu.SemaphoreType.DMA((count, parts - 1)),
+            pltpu.SemaphoreType.DMA((count,)),
+        ],
+        compiler_params=pltpu.CompilerParams(collective_id=name_id, has_side_effects=True),
+        cost_estimate=pl.CostEstimate(
+            flops=0,
+            bytes_accessed=sum(shape.size * shape.dtype.itemsize for shape in shapes),
+            transcendentals=0,
+        ),
+    )(*arrays)
+
+
+def total(slots):
+    return jnp.sum(slots.astype(jnp.float32), axis=0)
+
+
+def gather_grid(local_piece, name_id=None):
+    if name_id is None:
+        tall = lax.all_gather(local_piece, "col", axis=0, tiled=True)
+        return lax.all_gather(tall, "row", axis=1, tiled=True)
+    (tall,) = exchange("col", [local_piece], [False], name_id)
+    (wide,) = exchange("row", [tall.reshape(-1, tall.shape[2])], [False], name_id + 1)
+    return jnp.concatenate([wide[part] for part in range(wide.shape[0])], axis=1)
 
 
 def norm_stats(values):
@@ -128,9 +196,10 @@
     def own_rows(whole):
         return lax.dynamic_slice_in_dim(whole, token_base, own_tokens, 0)
 
-    tokens_all = gather_grid(tokens)
+    tokens_all = gather_grid(tokens, 0)
     qkv_cols = lax.all_gather(w_qkv, "row", axis=0, tiled=True)
-    vectors_all = lax.all_gather(row_vectors, "row", axis=1, tiled=True)
+    (vector_slots,) = exchange("row", [row_vectors], [False], 14)
+    vectors_all = jnp.concatenate([vector_slots[part] for part in range(row_parts)], axis=1)
     out_whole = gather_grid(w_out)
     fc_cols = lax.all_gather(w_fc, "row", axis=0, tiled=True)
     grad_all = gather_grid(out_grad)
@@ -165,37 +234,73 @@
         "hqk,hke->hqe", prob_low, value, preferred_element_type=jnp.float32
     ).astype(low)
     attn_local = attended.transpose(1, 0, 2).reshape(token_count, heads_local * HD)
-    attn_all = lax.all_gather(attn_local, "col", axis=1, tiled=True)
-    resid_mid = resid_in + product(attn_all, out_whole, False) + bias_out
+    part_tokens = token_count // row_parts
+    part_base = lax.axis_index("row") * part_tokens
+
+    def part_rows(whole):
+        return lax.dynamic_slice_in_dim(whole, part_base, part_tokens, 0)
+
+    (attn_slots,) = exchange("col", [part_rows(attn_local)], [False], 2)
+    attn_part = jnp.concatenate([attn_slots[part] for part in range(col_parts)], axis=1)
+    resid_mid = part_rows(resid_in) + product(attn_part, out_whole, False) + bias_out
     mean_two, inv_two = norm_stats(resid_mid)
     unit_two = (resid_mid - mean_two) * inv_two
     act_two = (unit_two * gain_two + shift_two).astype(low)
     hidden_pre = product(act_two, fc_cols, False) + bias_fc
     hidden = gelu_value(hidden_pre).astype(low)
-    grad_hidden = product(grad_all, proj_cols, False)
+    grad_part = part_rows(grad_all)
+    grad_hidden = product(grad_part, proj_cols, False)
     grad_pre = (gelu_slope(hidden_pre) * grad_hidden).astype(low)
 
-    grad_norm_two = lax.psum_scatter(
-        product(grad_pre, w_fc, True).astype(low), "col", scatter_dimension=0, tiled=True
-    )
-    grad_two_all = gather_grid(grad_norm_two).astype(jnp.float32)
-    grad_norm_two = grad_norm_two.astype(jnp.float32)
-    scaled = grad_two_all * gain_two
+    piece_tokens = part_tokens // col_parts
+    piece_base = lax.axis_index("col") * piece_tokens
+
+    def piece_rows(part):
+        return lax.dynamic_slice_in_dim(part, piece_base, piece_tokens, 0)
+
+    (two_slots,) = exchange(
+        "col",
+        [product(grad_pre, fc_cols, True).astype(low).reshape(col_parts, piece_tokens, -1)],
+        [True],
+        3,
+    )
+    grad_norm_two = total(two_slots)
+    unit_two_piece = piece_rows(unit_two)
+    scaled = grad_norm_two * gain_two
     first_mean = jnp.mean(scaled, axis=1, keepdims=True)
-    second_mean = jnp.mean(scaled * unit_two, axis=1, keepdims=True)
-    grad_mid_all = grad_all.astype(jnp.float32) + inv_two * (
-        scaled - first_mean - unit_two * second_mean
-    )
-    grad_mid_low = grad_mid_all.astype(low)
+    second_mean = jnp.mean(scaled * unit_two_piece, axis=1, keepdims=True)
+    grad_mid_piece = piece_rows(grad_part).astype(jnp.float32) + piece_rows(inv_two) * (
+        scaled - first_mean - unit_two_piece * second_mean
+    )
+    grad_mid_low = grad_mid_piece.astype(low)
+    (mid_slots,) = exchange("col", [grad_mid_low], [False], 4)
+    mid_part = mid_slots.reshape(part_tokens, feature_count)
     out_rows = lax.dynamic_slice_in_dim(
         out_whole, lax.axis_index("col") * w_out.shape[0], w_out.shape[0], 0
     )
+    grad_attn_part = product(mid_part, out_rows, True).astype(low)
+    split = lambda rows: rows.reshape(part_tokens, row_parts, own_features).transpose(1, 0, 2)
+    attn_grad_slots, mid_cols, act_two_cols, hidden_slots, grad_pre_slots, resid_cols = exchange(
+        "row",
+        [
+            grad_attn_part,
+            split(mid_part),
+            split(act_two),
+            hidden,
+            grad_pre,
+            split(resid_mid),
+        ],
+        [False, True, True, False, False, True],
+        5,
+    )
     grad_attn = (
-        product(grad_mid_low, out_rows, True)
-        .astype(low)
-        .reshape(token_count, heads_local, HD)
-        .transpose(1, 0, 2)
-    )
+        attn_grad_slots.reshape(token_count, heads_local, HD).transpose(1, 0, 2)
+    )
+    mid_cols = mid_cols.reshape(token_count, own_features)
+    act_two_cols = act_two_cols.reshape(token_count, own_features)
+    resid_cols = resid_cols.reshape(token_count, own_features)
+    hidden_all = hidden_slots.reshape(token_count, -1)
+    grad_pre_all = grad_pre_slots.reshape(token_count, -1)
 
     grad_value = jnp.einsum(
         "hqk,hqe->hke", prob_low, grad_attn, preferred_element_type=jnp.float32
@@ -215,19 +320,26 @@
 
     grad_blocks = (
         inner_rows(own_columns(act_one), grad_qkv_low),
-        inner_rows(attn_local, own_columns(grad_mid_low)),
-        inner_rows(own_columns(act_two), grad_pre),
-        inner_rows(hidden, own_columns(grad_all)),
-    )
-    summed = [lax.psum(block.astype(low), "dp").astype(jnp.float32) for block in grad_blocks]
-    bias_sums = lax.psum(
-        (
+        inner_rows(attn_local, mid_cols),
+        inner_rows(act_two_cols, grad_pre_all),
+        inner_rows(hidden_all, own_columns(grad_all)),
+    )
+    bias_blocks = jnp.concatenate(
+        [
             jnp.sum(grad_qkv_low, axis=0, dtype=jnp.float32),
-            jnp.sum(grad_pre, axis=0, dtype=jnp.float32),
-        ),
-        "dp",
-    )
-    summed = summed + list(bias_sums)
+            jnp.sum(grad_pre_all, axis=0, dtype=jnp.float32),
+        ]
+    )[None]
+    if dp_parts == 2:
+        group_slots = exchange(
+            "dp", [block.astype(low) for block in grad_blocks] + [bias_blocks], [False] * 5, 6
+        )
+        summed = [total(slots) for slots in group_slots]
+    else:
+        summed = [lax.psum(block.astype(low), "dp").astype(jnp.float32) for block in grad_blocks]
+        summed.append(lax.psum(bias_blocks, "dp"))
+    bias_sums = summed.pop()[0]
+    summed = summed + [bias_sums[: bias_qkv.shape[0]], bias_sums[bias_qkv.shape[0] :]]
 
     weights = (w_qkv, w_out, w_fc, w_proj)
     moments = (mom_qkv, mom_out, mom_fc, mom_proj)
@@ -247,21 +359,41 @@
         ]
     )
     outgoing = lax.dynamic_slice_in_dim(outgoing, lax.axis_index("dp") * share, share, 2)
-    arrived = lax.all_to_all(outgoing, "row", split_axis=0, concat_axis=0, tiled=True)
+    (arrived,) = exchange("row", [outgoing], [True], 7)
     matrix = arrived.reshape(feature_count, share)
-    gram = lax.psum(product(matrix, matrix, True).astype(low), ("dp", "col")).astype(jnp.float32)
+    gram_low = product(matrix, matrix, True).astype(low)
+    if dp_parts == 2:
+        (half_slots,) = exchange(
+            "dp", [gram_low.reshape(dp_parts, -1, feature_count)], [True], 8
+        )
+        gram_half = total(half_slots).astype(low)
+    else:
+        gram_half = lax.psum_scatter(gram_low, "dp", scatter_dimension=0, tiled=True)
+    if gram_half.shape[0] % (8 * col_parts) == 0:
+        (quarter_slots,) = exchange(
+            "col", [gram_half.reshape(col_parts, -1, feature_count)], [True], 9
+        )
+        (whole_slots,) = exchange("col", [total(quarter_slots).astype(low)], [False], 10)
+        gram_half = whole_slots.reshape(gram_half.shape)
+    else:
+        gram_half = lax.psum(gram_half, "col")
+    if dp_parts == 2:
+        (gram_slots,) = exchange("dp", [gram_half], [False], 11)
+        gram = gram_slots.reshape(feature_count, feature_count).astype(jnp.float32)
+    else:
+        gram = lax.all_gather(gram_half, "dp", axis=0, tiled=True).astype(jnp.float32)
     factor, scale, gram_norm = polynomial_factor(gram)
     ortho = (scale * matrix.astype(jnp.float32) + matrix_product(factor, matrix)) * lax.rsqrt(
         gram_norm
     )
-    back = lax.all_to_all(
-        ortho.astype(low).reshape(row_parts, own_features, share),
-        "row",
-        split_axis=0,
-        concat_axis=0,
-        tiled=True,
-    )
-    orthos = lax.all_gather(back, "dp", axis=2, tiled=True)
+    (back,) = exchange(
+        "row", [ortho.astype(low).reshape(row_parts, own_features, share)], [True], 12
+    )
+    if dp_parts == 2:
+        (ortho_slots,) = exchange("dp", [back], [False], 13)
+        orthos = jnp.concatenate([ortho_slots[part] for part in range(dp_parts)], axis=2)
+    else:
+        orthos = lax.all_gather(back, "dp", axis=2, tiled=True)
     new_weights = []
     for member in range(4):
         piece = orthos[member, :, : upright[member].shape[1]]
@@ -275,36 +407,55 @@
             - rate_matrix * math.sqrt(longest) * piece.astype(jnp.float32)
         )
 
-    block_sum = lax.psum_scatter(
-        product(hidden, proj_flip, True).astype(low), "col", scatter_dimension=0, tiled=True
-    ).astype(jnp.float32)
-    block_out = (own_block(resid_mid) + block_sum + row_vectors[5]).astype(low)
-    grad_norm_one = lax.psum_scatter(
-        product(grad_qkv_low, w_qkv, True).astype(low), "col", scatter_dimension=0, tiled=True
-    ).astype(jnp.float32)
+    outward = product(hidden_all, proj_flip, True).astype(low)
+    inward = product(grad_qkv_low, w_qkv, True).astype(low)
+    block_slots, one_slots = exchange(
+        "col",
+        [
+            outward.reshape(col_parts, own_tokens, own_features),
+            inward.reshape(col_parts, own_tokens, own_features),
+        ],
+        [True, True],
+        15,
+    )
+    block_out = (own_rows(resid_cols) + total(block_slots) + row_vectors[5]).astype(low)
+    grad_norm_one = total(one_slots)
     unit_one_own = own_block(unit_one)
     scaled_one = grad_norm_one * row_vectors[0]
-    first_sum, second_sum = lax.psum(
-        (
-            jnp.sum(scaled_one, axis=1, keepdims=True),
-            jnp.sum(scaled_one * unit_one_own, axis=1, keepdims=True),
-        ),
+    stat_pair = jnp.stack(
+        [jnp.sum(scaled_one, axis=1), jnp.sum(scaled_one * unit_one_own, axis=1)]
+    )
+    wide_terms = jnp.stack(
+        [
+            jnp.sum(grad_norm_two * unit_two_piece, axis=0),
+            jnp.sum(grad_norm_two, axis=0),
+        ]
+    )
+    stat_slots, wide_slots = exchange(
         "row",
-    )
-    input_grad = own_block(grad_mid_all) + own_rows(inv_one) * (
+        [stat_pair, wide_terms.reshape(2, row_parts, own_features).transpose(1, 0, 2)],
+        [False, True],
+        16,
+    )
+    stat_sum = total(stat_slots)
+    first_sum, second_sum = stat_sum[0][:, None], stat_sum[1][:, None]
+    wide_sum = total(wide_slots)
+    input_grad = own_rows(mid_cols).astype(jnp.float32) + own_rows(inv_one) * (
         scaled_one - first_sum / feature_count - unit_one_own * (second_sum / feature_count)
     )
     row_terms = jnp.stack(
         [
             jnp.sum(grad_norm_one * unit_one_own, axis=0),
             jnp.sum(grad_norm_one, axis=0),
-            jnp.sum(grad_norm_two * own_block(unit_two), axis=0),
-            jnp.sum(grad_norm_two, axis=0),
-            jnp.sum(own_block(grad_mid_low), axis=0, dtype=jnp.float32),
+            wide_sum[0],
+            wide_sum[1],
+            jnp.sum(own_rows(mid_cols), axis=0, dtype=jnp.float32),
             jnp.sum(out_grad, axis=0, dtype=jnp.float32),
         ]
     )
-    grad_rows = lax.psum(row_terms, ("dp", "col"))
+    (term_slots,) = exchange("col", [row_terms], [False], 17)
+    (pair_slots,) = exchange("dp", [total(term_slots)], [False], 18)
+    grad_rows = total(pair_slots)
     vector_rate = rate_vector / math.sqrt(token_count * dp_parts)
 
     def vector_step(weight, gradient, moment):

time: 444 us -> 396 us (0.89)
  Pallas kernels: 0 us -> 193 us
  blocking collectives: 213 us -> 56.4 us
  waiting for transfers between devices: 92.2 us -> 1.4 us
  other arithmetic: 32 us -> 47.1 us
  matrix products: 49.5 us -> 41.6 us
    pallas_call x0 -> x19, Pallas kernels: none -> 193 us  [exchange(): pl.pallas_call(functools.partial(exchange_kernel, axis, parts, tuple(kind...]
    all_gather x5 -> x3, blocking collectives: 159 us -> 44.5 us  [the longest x2 29.4 us: gather_grid(): tall = lax.all_gather(local_piece, 'col', axis=0, tiled=True)]
    psum x2 -> x0, waiting for transfers between devices: 66.2 us -> none  [the longest x1 50.5 us: local(): lax.psum(product(matrix, matrix, True).astype(low), ('dp', 'col'))]
    psum x3 -> x0, blocking collectives: 26.9 us -> none  [the longest x1 14.4 us: local(): grad_rows = lax.psum(row_terms, ('dp', 'col'))]
    reduce_scatter x3 -> x0, waiting for transfers between devices: 23.3 us -> none  [the longest x1 12.3 us: local(): lax.psum_scatter(product(grad_pre, w_fc, True).astype(low), 'col', scatte...]
    all_to_all x1 -> x0, blocking collectives: 13.6 us -> none  [local(): lax.all_to_all(outgoing, 'row', split_axis=0, concat_axis=0, tiled=True)]
    reduce_sum x3 -> x16, other arithmetic: 2.21 us -> 15.6 us  [the longest x12 12.2 us: total(): return jnp.sum(slots.astype(jnp.float32), axis=0)]
    unnamed x105 -> x120, local copies, waits for them, and re-layouts: 16.8 us -> 10.3 us
  transfers between devices with their start and end apart: 10 -> 3, of which waited for: 5 -> 0; matrix products, arithmetic and copies ran while one was open for 17% -> 9% of each run, Pallas kernels for 0% -> 11%
where the time goes in v2:
time: 396 us; the launch traced here: 393 us
  Pallas kernels  193 us (49%)
  blocking collectives  56.4 us (14%)
  other arithmetic  47.1 us (12%)
  matrix products  41.6 us (11%)
  local copies, waits for them, and re-layouts  37.9 us (10%)
  between operations  15.4 us (4%)
    pallas_call x19, Pallas kernels, exchange(): pl.pallas_call(functools.partial(exchange_kernel, axis, parts, tuple(kind...  193 us
    all_gather x2, blocking collectives, gather_grid(): tall = lax.all_gather(local_piece, 'col', axis=0, tiled=True)  29.4 us
    all_gather x1, blocking collectives, gather_grid(): return lax.all_gather(tall, 'row', axis=1, tiled=True)  15.2 us
    dot_general x5, matrix products, matrix_product(): jnp.dot(left_side.astype(jnp.bfloat16), right_side.astype(jnp.bfloat16),...  12.6 us
    reduce_sum x12, other arithmetic, total(): return jnp.sum(slots.astype(jnp.float32), axis=0)  12.2 us
    all_gather x1, blocking collectives, local(): qkv_cols = lax.all_gather(w_qkv, 'row', axis=0, tiled=True)  11.9 us
    unnamed x120, local copies, waits for them, and re-layouts  10.3 us
    dot_general x5, matrix products, product(): lax.dot_general(left_side, right_side, (((1,), (1,)), ((), ())), preferre...  8.06 us
  transfers between devices with their start and end apart: 3, of which 0 were waited for; matrix products, arithmetic and copies ran while one was open for 9% of the time, Pallas kernels for 11%

profile of v2, /device:TPU:0, one launch (start us, length us, event | category | flops | bytes accessed | tf_op | source)
XLA Modules:
  0.0 393.3 jit_solution(2833488993995166649)
XLA Ops:
  7.3 16.5 %all_gather.24 = bf16[768,192]{1,0:T(8,128)(2,1)S(1)} all-gather(bf16[192,192]{1,0:T(8,128)(2,1)} %param.21), channel_id=1, replica_groups=mesh['dp'=2,'row'=4,'col'=4] {'col'}, dimensions={0}, use_global_device_ids=true | all-gather | bytes 368640 | tf_op jit(solution)/shard_map/all_gather | solution.py:119
  26.9 12.9 %all_gather.21 = bf16[512,192]{0,1:T(8,128)(2,1)S(1)} all-gather(bf16[128,192]{0,1:T(8,128)(2,1)S(1)} %copy-done.30), channel_id=1, replica_groups=mesh['dp'=2,'row'=4,'col'=4] {'col'}, dimensions={0}, use_global_device_ids=true | all-gather | bytes 245760 | tf_op jit(solution)/shard_map/all_gather | solution.py:119
  39.8 15.2 %all_gather.22 = bf16[512,768]{0,1:T(8,128)(2,1)S(1)} all-gather(bf16[512,192]{0,1:T(8,128)(2,1)S(1)} %all_gather.21), channel_id=1, replica_groups=mesh['dp'=2,'row'=4,'col'=4] {'row'}, dimensions={1}, use_global_device_ids=true | all-gather | bytes 983040 | tf_op jit(solution)/shard_map/all_gather | solution.py:120
  54.9 6.2 %shard_map.349 = f32[4,6,192]{2,1,0:T(8,128)} custom-call(f32[6,192]{1,0:T(8,128)} %refs_0_.2), custom_call_target="tpu_custom_call" | custom-call | bytes 18432 | tf_op jit(solution)/shard_map/pallas_call | solution.py:94
  62.9 9.0 %shard_map.347 = bf16[4,128,192]{2,1,0:T(8,128)(2,1)} custom-call(bf16[128,192]{1,0:T(8,128)(2,1)} %copy.192.refs_0_), custom_call_target="tpu_custom_call" | custom-call | bytes 196608 | tf_op jit(solution)/shard_map/pallas_call | solution.py:94
  71.9 18.4 %shard_map.348 = bf16[4,512,192]{2,1,0:T(8,128)(2,1)} custom-call(bf16[512,192]{1,0:T(8,128)(2,1)} %bitcast.201), custom_call_target="tpu_custom_call" | custom-call | bytes 786432 | tf_op jit(solution)/shard_map/pallas_call | solution.py:94
  91.6 11.9 %all_gather.23 = bf16[768,576]{1,0:T(8,128)(2,1)S(1)} all-gather(bf16[192,576]{1,0:T(8,128)(2,1)S(1)} %copy-done.9), channel_id=1, replica_groups=mesh['dp'=2,'row'=4,'col'=4] {'row'}, dimensions={0}, use_global_device_ids=true | all-gather | bytes 1105920 | tf_op jit(solution)/shard_map/all_gather | solution.py:200
  108.6 2.9 fusion.67
  111.5 2.3 fusion.10
  116.9 9.2 %shard_map.350 = bf16[4,128,192]{2,1,0:T(8,128)(2,1)} custom-call(bf16[128,192]{1,0:T(8,128)(2,1)} %copy.232.refs_0_), custom_call_target="tpu_custom_call" | custom-call | bytes 196608 | tf_op jit(solution)/shard_map/pallas_call | solution.py:94
  127.4 1.7 copy.214
  133.5 2.8 fusion.65
  136.4 1.9 copy.200
  138.3 1.9 add_convert_fusion.4
  140.2 1.7 copy.198
  142.0 2.6 multiply_convert_fusion.1
  144.6 1.9 fusion.16.refs_4_
  147.7 8.7 %shard_map.351 = bf16[4,32,768]{2,1,0:T(8,128)(2,1)} custom-call(bf16[4,32,768]{2,1,0:T(8,128)(2,1)} %bitcast.207), custom_call_target="tpu_custom_call" | custom-call | bytes 196608 | tf_op jit(solution)/shard_map/pallas_call | solution.py:94
  160.1 8.5 %shard_map.352 = bf16[4,32,768]{2,1,0:T(8,128)(2,1)} custom-call(bf16[32,768]{1,0:T(8,128)(2,1)} %add_convert_fusion.7.refs_0_), custom_call_target="tpu_custom_call" | custom-call | bytes 196608 | tf_op jit(solution)/shard_map/pallas_call | solution.py:94
  168.5 1.9 reshape_reshape.3
  170.4 1.7 convolution_convert_fusion.11
  174.6 1.8 copy.199
  176.3 2.0 copy.201
  178.3 23.6 %shard_map.353 = (bf16[4,128,192]{2,1,0:T(8,128)(2,1)}, bf16[4,128,192]{2,1,0:T(8,128)(2,1)}, bf16[4,128,192]{2,1,0:T(8,128)(2,1)}, bf16[4,128,768]{2,1,0:T(8,12...) custom-call(bf16[128,192]{1,0:T(8,128)(2,1)} %copy.202.refs_0_, bf16[4,128,192]{2,1,0:T(8,128)(2,1)} %bitcast.205, ...), custom_call_target="tpu_custom_call" | custom-call | bytes 2555904 | tf_op jit(solution)/shard_map/pallas_call | solution.py:94
  202.0 1.8 copy.204
  207.1 2.6 multiply_convert_fusion
  213.2 2.3 convolution_convert_fusion.2.refs_0_
  219.6 5.4 %shard_map.356 = (bf16[2,192,576]{2,1,0:T(8,128)(2,1)}, bf16[2,192,192]{2,1,0:T(8,128)(2,1)}, bf16[2,192,768]{2,1,0:T(8,128)(2,1)}, bf16[2,768,192]{2,1,0:T(8,128)(2,1)}, f32[2,1,1344]{2,1,0:T(1,128)}) custom-call(bf16[192,576]{1,0:T(8,128)(2,1)} %convolution_convert_fusion.2.refs_0_, bf16[192,192]{1,0:T(8,128)(2,1)} %convolution_convert_fusion.10.refs_1_, ...), custom_call_target="tpu_custom_call" | custom-call | bytes 1780224 | tf_op jit(solution)/shard_map/pallas_call | solution.py:94
  228.9 2.1 add_convert_fusion.3
  234.7 12.0 %shard_map.359 = bf16[4,192,384]{2,1,0:T(8,128)(2,1)} custom-call(bf16[4,192,384]{2,1,0:T(8,128)(2,1)} %fusion.26.refs_0_), custom_call_target="tpu_custom_call" | custom-call | bytes 589824 | tf_op jit(solution)/shard_map/pallas_call | solution.py:94
  246.7 3.1 convolution_convert_fusion
  249.8 4.3 %shard_map.360 = bf16[2,384,768]{2,1,0:T(8,128)(2,1)} custom-call(bf16[2,384,768]{2,1,0:T(8,128)(2,1)} %bitcast.185), custom_call_target="tpu_custom_call" | custom-call | bytes 1179648 | tf_op jit(solution)/shard_map/pallas_call | solution.py:94
  254.1 2.5 reduce_sum.339
  256.6 16.1 %shard_map.361 = bf16[4,96,768]{2,1,0:T(8,128)(2,1)} custom-call(bf16[4,96,768]{2,1,0:T(8,128)(2,1)} %bitcast.190), custom_call_target="tpu_custom_call" | custom-call | bytes 589824 | tf_op jit(solution)/shard_map/pallas_call | solution.py:94
  272.7 1.9 reduce_sum.340.refs_0_
  274.5 18.0 %shard_map.362 = bf16[4,96,768]{2,1,0:T(8,128)(2,1)} custom-call(bf16[96,768]{1,0:T(8,128)(2,1)} %reduce_sum.340.refs_0_), custom_call_target="tpu_custom_call" | custom-call | bytes 589824 | tf_op jit(solution)/shard_map/pallas_call | solution.py:94
  292.6 4.1 %shard_map.363 = bf16[2,384,768]{2,1,0:T(8,128)(2,1)} custom-call(bf16[384,768]{1,0:T(8,128)(2,1)} %bitcast.189), custom_call_target="tpu_custom_call" | custom-call | bytes 1179648 | tf_op jit(solution)/shard_map/pallas_call | solution.py:94
  296.7 2.6 fusion.2
  300.0 2.6 broadcast_multiply_fusion
  302.7 2.9 bitcast_add_fusion.1
  307.8 2.5 multiply_add_fusion.1
  310.4 4.9 %fusion.9 = bf16[768,384]{1,0:T(8,128)(2,1)} fusion(bf16[768,384]{1,0:T(8,128)(2,1)S(1)} %bitcast.180, f32[768,768]{1,0:T(8,128)S(1)} %bitcast_add_fusion.1, f32[768,768]{1,0:T(8,128)} %multiply_add_fusion.1, f32[]{:T(128)S(6)} %rsqrt.35), kind=kOutput, calls=%fused_computation.28 | convolution fusion | flops 1363968000 | bytes 5898244 | tf_op jit(solution)/shard_map/dot_general | solution.py:134
  315.3 11.9 %shard_map.364.refs_0_ = bf16[4,192,384]{2,1,0:T(8,128)(2,1)} custom-call(bf16[4,192,384]{2,1,0:T(8,128)(2,1)} %bitcast.208), custom_call_target="tpu_custom_call" | custom-call | bytes 589824 | tf_op jit(solution)/shard_map/pallas_call | solution.py:94
  327.2 4.1 %shard_map.365 = bf16[2,4,192,384]{3,2,1,0:T(8,128)(2,1)} custom-call(bf16[4,192,384]{2,1,0:T(8,128)(2,1)} %shard_map.364.refs_0_), custom_call_target="tpu_custom_call" | custom-call | bytes 1179648 | tf_op jit(solution)/shard_map/pallas_call | solution.py:94
  337.2 17.9 %shard_map.354 = (bf16[4,128,192]{2,1,0:T(8,128)(2,1)}, bf16[4,128,192]{2,1,0:T(8,128)(2,1)}) custom-call(bf16[4,128,192]{2,1,0:T(8,128)(2,1)} %bitcast.202, bf16[4,128,192]{2,1,0:T(8,128)(2,1)} %bitcast.203), custom_call_target="tpu_custom_call" | custom-call | bytes 393216 | tf_op jit(solution)/shard_map/pallas_call | solution.py:94
  361.4 6.0 %shard_map.355 = (f32[4,2,128]{2,1,0:T(2,128)}, f32[4,2,192]{2,1,0:T(2,128)}) custom-call(f32[2,128]{1,0:T(2,128)} %pad_maximum_fusion.6.refs_0_, f32[4,2,192]{2,1,0:T(2,128)} %maximum_bitcast_fusion.1.refs_1_), custom_call_target="tpu_custom_call" | custom-call | bytes 10240 | tf_op jit(solution)/shard_map/pallas_call | solution.py:94
  371.3 7.4 %shard_map.357 = f32[4,6,192]{2,1,0:T(8,128)} custom-call(f32[6,192]{1,0:T(8,128)} %stack.74.refs_0_), custom_call_target="tpu_custom_call" | custom-call | bytes 18432 | tf_op jit(solution)/shard_map/pallas_call | solution.py:94
  380.0 2.5 shard_map.358
  (214 shorter events, 69.2 us)
Async XLA Ops:
  7.2 18.9 %copy-start.28 = (bf16[192,192]{1,0:T(8,128)(2,1)S(1)}, bf16[192,192]{1,0:T(8,128)(2,1)}, u32[]{:S(2)}) copy-start(bf16[192,192]{1,0:T(8,128)(2,1)} %param.21) | copy-start | bytes 221188
  7.2 19.7 %copy-start.30 = (bf16[128,192]{0,1:T(8,128)(2,1)S(1)}, bf16[128,192]{0,1:T(8,128)(2,1)}, u32[]{:S(2)}) copy-start(bf16[128,192]{0,1:T(8,128)(2,1)} %param.18) | copy-start | bytes 147460
  7.2 126.3 %all-gather.4.cloned.1.call-start = ((), (), s32[]{:S(2)}) async-start(), calls=%async_computation | async-start | bytes 1474560 | tf_op jit(solution)/shard_map/all_gather | solution.py:120
  23.7 38.2 %copy-start.42 = (s32[1,512]{1,0:T(1,128)S(1)}, s32[1,512]{1,0:T(1,128)}, u32[]{:S(2)}) copy-start(s32[1,512]{1,0:T(1,128)} %param.19) | copy-start | bytes 6148
  23.7 38.4 %copy-start.34 = (bf16[128,192]{0,1:T(8,128)(2,1)S(1)}, bf16[128,192]{0,1:T(8,128)(2,1)}, u32[]{:S(2)}) copy-start(bf16[128,192]{0,1:T(8,128)(2,1)} %param.17) | copy-start | bytes 147460
  24.6 117.3 %all-gather.6.cloned.1.call-start = ((), (), s32[]{:S(2)}) async-start(), calls=%async_computation.1 | async-start | bytes 1474560 | tf_op jit(solution)/shard_map/all_gather | solution.py:204
  25.4 119.2 %all-gather.8.cloned.1.call-start = ((), (), s32[]{:S(2)}) async-start(), calls=%async_computation.2 | async-start | bytes 1474560 | tf_op jit(solution)/shard_map/all_gather | solution.py:207
  61.9 43.5 %copy-start.31 = (f32[6,192]{1,0:T(8,128)}, f32[6,192]{1,0:T(8,128)S(1)}, u32[]{:S(2)}) copy-start(f32[6,192]{1,0:T(8,128)S(1)} %get-tuple-element.247) | copy-start | bytes 13828
  61.9 43.5 %copy-start.32 = (f32[6,192]{1,0:T(8,128)}, f32[6,192]{1,0:T(8,128)S(1)}, u32[]{:S(2)}) copy-start(f32[6,192]{1,0:T(8,128)S(1)} %get-tuple-element.248) | copy-start | bytes 13828
  71.9 19.7 %copy-start.9 = (bf16[192,576]{1,0:T(8,128)(2,1)S(1)}, bf16[192,576]{1,0:T(8,128)(2,1)}, u32[]{:S(2)}) copy-start(bf16[192,576]{1,0:T(8,128)(2,1)} %param.20) | copy-start | bytes 663556
  105.4 2.2 copy-start.43
  111.5 2.3 copy-start.40
  133.5 4.8 %copy-start.33 = (f32[768]{0:T(1024)S(1)}, f32[768]{0:T(1024)}, u32[]{:S(2)}) copy-start(f32[768]{0:T(1024)} %get-tuple-element.205) | copy-start | bytes 9220
  136.3 5.7 %copy-start.50 = (f32[768]{0:T(1024)S(1)}, f32[768]{0:T(1024)}, u32[]{:S(2)}) copy-start(f32[768]{0:T(1024)} %param.25) | copy-start | bytes 9220
  144.5 1.9 copy-start.14
  201.9 5.2 %copy-start.41 = (f32[3,512]{1,0:T(4,128)S(1)}, f32[3,512]{1,0:T(4,128)}, u32[]{:S(2)}) copy-start(f32[3,512]{1,0:T(4,128)} %copy-done.40) | copy-start | bytes 18436
  212.2 3.7 copy-start.26
  213.2 3.5 copy-start.4
  225.0 3.4 copy-start.23
  225.0 3.5 copy-start.17
  225.9 159.0 %copy-start.38 = (f32[576]{0:T(1024)}, f32[576]{0:T(1024)S(1)}, u32[]{:S(2)}) copy-start(f32[576]{0:T(1024)S(1)} %slice_reduce_fusion.1) | copy-start | bytes 6916
  226.0 159.5 %copy-start.37 = (f32[768]{0:T(1024)}, f32[768]{0:T(1024)S(1)}, u32[]{:S(2)}) copy-start(f32[768]{0:T(1024)S(1)} %slice_reduce_fusion) | copy-start | bytes 9220
  227.2 1.7 copy-start.11
  228.3 2.8 copy-start.18
  228.5 3.5 copy-start.7
  228.9 4.0 %copy-start.8 = (f32[768,192]{0,1:T(8,128)}, f32[768,192]{0,1:T(8,128)S(1)}, u32[]{:S(2)}) copy-start(f32[768,192]{0,1:T(8,128)S(1)} %copy.222) | copy-start | bytes 1769476
  228.9 2.3 copy-start.19
  228.9 3.1 copy-start.24
  296.7 3.3 copy-start
  302.7 2.9 copy-start.1
  307.8 2.6 copy-start.2
  331.4 2.3 copy-start.15
  332.8 1.8 copy-start.6
  333.7 1.8 copy-start.16
  334.6 1.8 copy-start.21
  334.6 21.5 %copy-start.45 = (f32[1,192]{1,0:T(1,128)S(1)}, f32[1,192]{1,0:T(1,128)}, u32[]{:S(2)}) copy-start(f32[1,192]{1,0:T(1,128)} %get-tuple-element.250) | copy-start | bytes 2308
  335.5 23.6 %copy-start.39 = (f32[1,192]{1,0:T(1,128)S(1)}, f32[1,192]{1,0:T(1,128)}, u32[]{:S(2)}) copy-start(f32[1,192]{1,0:T(1,128)} %get-tuple-element.249) | copy-start | bytes 2308
  335.5 32.6 %copy-start.53 = (f32[128]{0:T(128)S(1)}, f32[128]{0:T(128)}, u32[]{:S(2)}) copy-start(f32[128]{0:T(128)} %dynamic-slice.1) | copy-start | bytes 1540
  336.3 34.3 %copy-start.46 = (f32[192]{0:T(256)S(1)}, f32[192]{0:T(256)}, u32[]{:S(2)}) copy-start(f32[192]{0:T(256)} %convert_reduce_fusion.13) | copy-start | bytes 2308
  337.2 46.1 %copy-start.27 = (bf16[192,192]{0,1:T(8,128)(2,1)S(1)}, bf16[192,192]{0,1:T(8,128)(2,1)}, u32[]{:S(2)}) copy-start(bf16[192,192]{0,1:T(8,128)(2,1)} %copy.219) | copy-start | bytes 221188
  355.0 29.0 %copy-start.20 = (f32[192,192]{0,1:T(8,128)S(1)}, f32[192,192]{0,1:T(8,128)}, u32[]{:S(2)}) copy-start(f32[192,192]{0,1:T(8,128)} %get-tuple-element.237) | copy-start | bytes 442372
  356.1 28.8 %copy-start.48 = (f32[576]{0:T(1024)S(1)}, f32[576]{0:T(1024)}, u32[]{:S(2)}) copy-start(f32[576]{0:T(1024)} %param.24) | copy-start | bytes 6916
  356.1 28.8 %copy-start.49 = (f32[576]{0:T(1024)S(1)}, f32[576]{0:T(1024)}, u32[]{:S(2)}) copy-start(f32[576]{0:T(1024)} %param.31) | copy-start | bytes 6916
  356.1 29.4 %copy-start.51 = (f32[768]{0:T(1024)S(1)}, f32[768]{0:T(1024)}, u32[]{:S(2)}) copy-start(f32[768]{0:T(1024)} %param.25) | copy-start | bytes 9220
  356.1 29.4 %copy-start.52 = (f32[768]{0:T(1024)S(1)}, f32[768]{0:T(1024)}, u32[]{:S(2)}) copy-start(f32[768]{0:T(1024)} %param.32) | copy-start | bytes 9220
  356.2 30.0 %copy-start.35 = (f32[6,192]{1,0:T(8,128)S(1)}, f32[6,192]{1,0:T(8,128)}, u32[]{:S(2)}) copy-start(f32[6,192]{1,0:T(8,128)} %refs_0_.2) | copy-start | bytes 13828
  356.2 29.9 %copy-start.44 = (f32[6,192]{1,0:T(8,128)S(1)}, f32[6,192]{1,0:T(8,128)}, u32[]{:S(2)}) copy-start(f32[6,192]{1,0:T(8,128)} %param.33) | copy-start | bytes 13828
  383.2 3.5 copy-start.36
  (9 other events, 12.1 us)
Sparse Core Ops, SparseCore 0:
  24.8 32.5 all-gather.3
  59.2 33.2 all-gather.5
  94.3 28.1 all-gather.7

commit v3 on v2

--- a/solution.py
+++ b/solution.py
@@ -44,22 +44,27 @@
     )
 
 
-def exchange_kernel(axis, parts, kinds, *refs):
+def exchange_kernel(axes, parts, kinds, *refs):
     count = len(kinds)
     sources, targets = refs[:count], refs[count : 2 * count]
     send_sem, recv_sem, local_sem = refs[2 * count :]
-    me = lax.axis_index(axis)
     barrier = pltpu.get_barrier_semaphore()
-    for step in range(1, parts):
-        peer = lax.rem(me + step, parts)
-        pl.semaphore_signal(
-            barrier, inc=1, device_id={axis: peer}, device_id_type=pl.DeviceIdType.MESH
-        )
-    pl.semaphore_wait(barrier, parts - 1)
+    met = 0
+    for axis in sorted(set(axes)):
+        axis_parts = parts[axes.index(axis)]
+        for step in range(1, axis_parts):
+            peer = lax.rem(lax.axis_index(axis) + step, axis_parts)
+            pl.semaphore_signal(
+                barrier, inc=1, device_id={axis: peer}, device_id_type=pl.DeviceIdType.MESH
+            )
+            met += 1
+    pl.semaphore_wait(barrier, met)
     copies = []
     for which in range(count):
-        for step in range(1, parts):
-            peer = lax.rem(me + step, parts)
+        axis = axes[which]
+        me = lax.axis_index(axis)
+        for step in range(1, parts[which]):
+            peer = lax.rem(me + step, parts[which])
             copy = pltpu.make_async_remote_copy(
                 src_ref=sources[which].at[peer] if kinds[which] else sources[which],
                 dst_ref=targets[which].at[me],
@@ -71,6 +76,7 @@
             copy.start()
             copies.append(copy)
     for which in range(count):
+        me = lax.axis_index(axes[which])
         copy = pltpu.make_async_copy(
             sources[which].at[me] if kinds[which] else sources[which],
             targets[which].at[me],
@@ -82,31 +88,26 @@
         copy.wait()
 
 
-def exchange(axis, arrays, kinds, name_id):
-    parts = lax.axis_size(axis)
+def exchange(axes, arrays, kinds, name_id):
     count = len(arrays)
+    if isinstance(axes, str):
+        axes = [axes] * count
+    parts = [lax.axis_size(axis) for axis in axes]
     shapes = [
-        jax.ShapeDtypeStruct(
-            array.shape if kind else (parts,) + array.shape, array.dtype
-        )
-        for array, kind in zip(arrays, kinds)
+        jax.ShapeDtypeStruct(array.shape if kind else (part,) + array.shape, array.dtype)
+        for array, kind, part in zip(arrays, kinds, parts)
     ]
     return pl.pallas_call(
-        functools.partial(exchange_kernel, axis, parts, tuple(kinds)),
+        functools.partial(exchange_kernel, tuple(axes), tuple(parts), tuple(kinds)),
         out_shape=shapes,
         in_specs=[pl.BlockSpec(memory_space=pltpu.VMEM)] * count,
         out_specs=[pl.BlockSpec(memory_space=pltpu.VMEM)] * count,
         scratch_shapes=[
-            pltpu.SemaphoreType.DMA((count, parts - 1)),
-            pltpu.SemaphoreType.DMA((count, parts - 1)),
+            pltpu.SemaphoreType.DMA((count, max(parts) - 1)),
+            pltpu.SemaphoreType.DMA((count, max(parts) - 1)),
             pltpu.SemaphoreType.DMA((count,)),
         ],
         compiler_params=pltpu.CompilerParams(collective_id=name_id, has_side_effects=True),
-        cost_estimate=pl.CostEstimate(
-            flops=0,
-            bytes_accessed=sum(shape.size * shape.dtype.itemsize for shape in shapes),
-            transcendentals=0,
-        ),
     )(*arrays)
 
 
@@ -114,13 +115,8 @@
     return jnp.sum(slots.astype(jnp.float32), axis=0)
 
 
-def gather_grid(local_piece, name_id=None):
-    if name_id is None:
-        tall = lax.all_gather(local_piece, "col", axis=0, tiled=True)
-        return lax.all_gather(tall, "row", axis=1, tiled=True)
-    (tall,) = exchange("col", [local_piece], [False], name_id)
-    (wide,) = exchange("row", [tall.reshape(-1, tall.shape[2])], [False], name_id + 1)
-    return jnp.concatenate([wide[part] for part in range(wide.shape[0])], axis=1)
+def side_by_side(slots):
+    return jnp.concatenate([slots[part] for part in range(slots.shape[0])], axis=1)
 
 
 def norm_stats(values):
@@ -196,15 +192,42 @@
     def own_rows(whole):
         return lax.dynamic_slice_in_dim(whole, token_base, own_tokens, 0)
 
-    tokens_all = gather_grid(tokens, 0)
-    qkv_cols = lax.all_gather(w_qkv, "row", axis=0, tiled=True)
-    (vector_slots,) = exchange("row", [row_vectors], [False], 14)
-    vectors_all = jnp.concatenate([vector_slots[part] for part in range(row_parts)], axis=1)
-    out_whole = gather_grid(w_out)
-    fc_cols = lax.all_gather(w_fc, "row", axis=0, tiled=True)
-    grad_all = gather_grid(out_grad)
     proj_flip = w_proj.T
-    proj_cols = lax.all_gather(proj_flip, "row", axis=0, tiled=True)
+    tokens_tall, grad_tall, out_tall = exchange(
+        "col", [tokens, out_grad, w_out.T], [False] * 3, 0
+    )
+    grad_cols = grad_tall.reshape(token_count, own_features)
+    matrices = [w_qkv, side_by_side(out_tall), w_fc, proj_flip]
+    halved = dp_parts == 2
+    pieces = matrices
+    if halved:
+        piece_size = own_features // 2
+        pieces = [
+            lax.dynamic_slice_in_dim(whole, lax.axis_index("dp") * piece_size, piece_size, 0)
+            for whole in matrices
+        ]
+    token_slots, grad_slots, vector_slots, *gathered = exchange(
+        "row",
+        [
+            tokens_tall.reshape(token_count, own_features),
+            grad_cols.reshape(row_parts, -1, own_features),
+            row_vectors,
+        ]
+        + pieces,
+        [False, True, False] + [False] * 4,
+        1,
+    )
+    if halved:
+        gathered = [
+            both.transpose(1, 0, 2, 3)
+            for both in exchange("dp", gathered, [False] * 4, 19)
+        ]
+    qkv_cols, out_flip, fc_cols, proj_cols = [
+        slots.reshape(feature_count, -1) for slots in gathered
+    ]
+    tokens_all = side_by_side(token_slots)
+    grad_part = side_by_side(grad_slots)
+    vectors_all = side_by_side(vector_slots)
     gain_one, shift_one, gain_two, shift_two, bias_out, _ = [
         vectors_all[which] for which in range(6)
     ]
@@ -242,13 +265,12 @@
 
     (attn_slots,) = exchange("col", [part_rows(attn_local)], [False], 2)
     attn_part = jnp.concatenate([attn_slots[part] for part in range(col_parts)], axis=1)
-    resid_mid = part_rows(resid_in) + product(attn_part, out_whole, False) + bias_out
+    resid_mid = part_rows(resid_in) + product(attn_part, out_flip, True) + bias_out
     mean_two, inv_two = norm_stats(resid_mid)
     unit_two = (resid_mid - mean_two) * inv_two
     act_two = (unit_two * gain_two + shift_two).astype(low)
     hidden_pre = product(act_two, fc_cols, False) + bias_fc
     hidden = gelu_value(hidden_pre).astype(low)
-    grad_part = part_rows(grad_all)
     grad_hidden = product(grad_part, proj_cols, False)
     grad_pre = (gelu_slope(hidden_pre) * grad_hidden).astype(low)
 
@@ -276,9 +298,9 @@
     (mid_slots,) = exchange("col", [grad_mid_low], [False], 4)
     mid_part = mid_slots.reshape(part_tokens, feature_count)
     out_rows = lax.dynamic_slice_in_dim(
-        out_whole, lax.axis_index("col") * w_out.shape[0], w_out.shape[0], 0
-    )
-    grad_attn_part = product(mid_part, out_rows, True).astype(low)
+        out_flip, lax.axis_index("col") * w_out.shape[0], w_out.shape[0], 1
+    )
+    grad_attn_part = product(mid_part, out_rows, False).astype(low)
     split = lambda rows: rows.reshape(part_tokens, row_parts, own_features).transpose(1, 0, 2)
     attn_grad_slots, mid_cols, act_two_cols, hidden_slots, grad_pre_slots, resid_cols = exchange(
         "row",
@@ -322,7 +344,7 @@
         inner_rows(own_columns(act_one), grad_qkv_low),
         inner_rows(attn_local, mid_cols),
         inner_rows(act_two_cols, grad_pre_all),
-        inner_rows(hidden_all, own_columns(grad_all)),
+        inner_rows(hidden_all, grad_cols),
     )
     bias_blocks = jnp.concatenate(
         [
@@ -359,29 +381,103 @@
         ]
     )
     outgoing = lax.dynamic_slice_in_dim(outgoing, lax.axis_index("dp") * share, share, 2)
-    (arrived,) = exchange("row", [outgoing], [True], 7)
+    outward = product(hidden_all, proj_flip, True).astype(low)
+    inward = product(grad_qkv_low, w_qkv, True).astype(low)
+    arrived, block_slots, one_slots = exchange(
+        ["row", "col", "col"],
+        [
+            outgoing,
+            outward.reshape(col_parts, own_tokens, own_features),
+            inward.reshape(col_parts, own_tokens, own_features),
+        ],
+        [True] * 3,
+        7,
+    )
     matrix = arrived.reshape(feature_count, share)
     gram_low = product(matrix, matrix, True).astype(low)
+    edge = feature_count // 3
+    spots = [(0, 0), (0, 1), (0, 2), (1, 1), (1, 2), (2, 2)]
+    packed = jnp.concatenate(
+        [
+            gram_low[up * edge : (up + 1) * edge, across * edge : (across + 1) * edge]
+            for up, across in spots
+        ],
+        axis=0,
+    )
+    block_out = (own_rows(resid_cols) + total(block_slots) + row_vectors[5]).astype(low)
+    grad_norm_one = total(one_slots)
+    unit_one_own = own_block(unit_one)
+    scaled_one = grad_norm_one * row_vectors[0]
+    stat_pair = jnp.stack(
+        [jnp.sum(scaled_one, axis=1), jnp.sum(scaled_one * unit_one_own, axis=1)]
+    )
+    wide_terms = jnp.stack(
+        [
+            jnp.sum(grad_norm_two * unit_two_piece, axis=0),
+            jnp.sum(grad_norm_two, axis=0),
+        ]
+    )
+    wide_slot_terms = wide_terms.reshape(2, row_parts, own_features).transpose(1, 0, 2)
     if dp_parts == 2:
-        (half_slots,) = exchange(
-            "dp", [gram_low.reshape(dp_parts, -1, feature_count)], [True], 8
+        stat_slots, wide_slots, half_slots = exchange(
+            ["row", "row", "dp"],
+            [stat_pair, wide_slot_terms, packed.reshape(dp_parts, -1, edge)],
+            [False, True, True],
+            8,
         )
         gram_half = total(half_slots).astype(low)
     else:
-        gram_half = lax.psum_scatter(gram_low, "dp", scatter_dimension=0, tiled=True)
-    if gram_half.shape[0] % (8 * col_parts) == 0:
-        (quarter_slots,) = exchange(
-            "col", [gram_half.reshape(col_parts, -1, feature_count)], [True], 9
-        )
-        (whole_slots,) = exchange("col", [total(quarter_slots).astype(low)], [False], 10)
-        gram_half = whole_slots.reshape(gram_half.shape)
+        stat_slots, wide_slots = exchange(
+            "row", [stat_pair, wide_slot_terms], [False, True], 8
+        )
+        gram_half = lax.psum(packed, "dp")
+    stat_sum = total(stat_slots)
+    first_sum, second_sum = stat_sum[0][:, None], stat_sum[1][:, None]
+    wide_sum = total(wide_slots)
+    input_grad = own_rows(mid_cols).astype(jnp.float32) + own_rows(inv_one) * (
+        scaled_one - first_sum / feature_count - unit_one_own * (second_sum / feature_count)
+    )
+    row_terms = jnp.stack(
+        [
+            jnp.sum(grad_norm_one * unit_one_own, axis=0),
+            jnp.sum(grad_norm_one, axis=0),
+            wide_sum[0],
+            wide_sum[1],
+            jnp.sum(own_rows(mid_cols), axis=0, dtype=jnp.float32),
+            jnp.sum(out_grad, axis=0, dtype=jnp.float32),
+        ]
+    )
+    quarter_slots, term_slots = exchange(
+        "col",
+        [gram_half.reshape(col_parts, -1, edge), row_terms],
+        [True, False],
+        9,
+    )
+    (whole_slots,) = exchange("col", [total(quarter_slots).astype(low)], [False], 10)
+    gram_half = whole_slots.reshape(gram_half.shape)
+    if dp_parts == 2:
+        gram_slots, pair_slots = exchange(
+            "dp", [gram_half, total(term_slots)], [False, False], 11
+        )
+        gram_half = gram_slots
     else:
-        gram_half = lax.psum(gram_half, "col")
-    if dp_parts == 2:
-        (gram_slots,) = exchange("dp", [gram_half], [False], 11)
-        gram = gram_slots.reshape(feature_count, feature_count).astype(jnp.float32)
-    else:
-        gram = lax.all_gather(gram_half, "dp", axis=0, tiled=True).astype(jnp.float32)
+        (pair_slots,) = exchange("dp", [total(term_slots)], [False], 11)
+    grad_rows = total(pair_slots)
+    tiles = gram_half.reshape(len(spots), edge, edge)
+    found = {spot: tiles[which] for which, spot in enumerate(spots)}
+    gram = jnp.concatenate(
+        [
+            jnp.concatenate(
+                [
+                    found[up, across] if across >= up else found[across, up].T
+                    for across in range(3)
+                ],
+                axis=1,
+            )
+            for up in range(3)
+        ],
+        axis=0,
+    ).astype(jnp.float32)
     factor, scale, gram_norm = polynomial_factor(gram)
     ortho = (scale * matrix.astype(jnp.float32) + matrix_product(factor, matrix)) * lax.rsqrt(
         gram_norm
@@ -407,55 +503,6 @@
             - rate_matrix * math.sqrt(longest) * piece.astype(jnp.float32)
         )
 
-    outward = product(hidden_all, proj_flip, True).astype(low)
-    inward = product(grad_qkv_low, w_qkv, True).astype(low)
-    block_slots, one_slots = exchange(
-        "col",
-        [
-            outward.reshape(col_parts, own_tokens, own_features),
-            inward.reshape(col_parts, own_tokens, own_features),
-        ],
-        [True, True],
-        15,
-    )
-    block_out = (own_rows(resid_cols) + total(block_slots) + row_vectors[5]).astype(low)
-    grad_norm_one = total(one_slots)
-    unit_one_own = own_block(unit_one)
-    scaled_one = grad_norm_one * row_vectors[0]
-    stat_pair = jnp.stack(
-        [jnp.sum(scaled_one, axis=1), jnp.sum(scaled_one * unit_one_own, axis=1)]
-    )
-    wide_terms = jnp.stack(
-        [
-            jnp.sum(grad_norm_two * unit_two_piece, axis=0),
-            jnp.sum(grad_norm_two, axis=0),
-        ]
-    )
-    stat_slots, wide_slots = exchange(
-        "row",
-        [stat_pair, wide_terms.reshape(2, row_parts, own_features).transpose(1, 0, 2)],
-        [False, True],
-        16,
-    )
-    stat_sum = total(stat_slots)
-    first_sum, second_sum = stat_sum[0][:, None], stat_sum[1][:, None]
-    wide_sum = total(wide_slots)
-    input_grad = own_rows(mid_cols).astype(jnp.float32) + own_rows(inv_one) * (
-        scaled_one - first_sum / feature_count - unit_one_own * (second_sum / feature_count)
-    )
-    row_terms = jnp.stack(
-        [
-            jnp.sum(grad_norm_one * unit_one_own, axis=0),
-            jnp.sum(grad_norm_one, axis=0),
-            wide_sum[0],
-            wide_sum[1],
-            jnp.sum(own_rows(mid_cols), axis=0, dtype=jnp.float32),
-            jnp.sum(out_grad, axis=0, dtype=jnp.float32),
-        ]
-    )
-    (term_slots,) = exchange("col", [row_terms], [False], 17)
-    (pair_slots,) = exchange("dp", [total(term_slots)], [False], 18)
-    grad_rows = total(pair_slots)
     vector_rate = rate_vector / math.sqrt(token_count * dp_parts)
 
     def vector_step(weight, gradient, moment):

time: 396 us -> 353 us (0.89)
  blocking collectives: 56.4 us -> 0 us
  Pallas kernels: 193 us -> 217 us
  between operations: 15.4 us -> 2.34 us
  local copies, waits for them, and re-layouts: 37.9 us -> 48.9 us
  matrix products: 41.6 us -> 37.1 us
    all_gather x4 -> x0, blocking collectives: 56.4 us -> none  [the longest x2 29.4 us: gather_grid(): tall = lax.all_gather(local_piece, 'col', axis=0, tiled=True)]
    pallas_call x19 -> x15, Pallas kernels: 193 us -> 217 us  [exchange(): pl.pallas_call(functools.partial(exchange_kernel, tuple(axes), tuple(part...]
    unnamed x120 -> x126, local copies, waits for them, and re-layouts: 10.3 us -> 18 us
  transfers between devices with their start and end apart: 3 -> 0, of which waited for: 0 -> 0; matrix products, arithmetic and copies ran while one was open for 9% -> 0% of each run, Pallas kernels for 11% -> 0%
where the time goes in v3:
time: 353 us; the launch traced here: 350 us
  Pallas kernels  217 us (61%)
  local copies, waits for them, and re-layouts  48.9 us (14%)
  other arithmetic  44.6 us (13%)
  matrix products  37.1 us (11%)
    pallas_call x15, Pallas kernels, exchange(): pl.pallas_call(functools.partial(exchange_kernel, tuple(axes), tuple(part...  217 us
    unnamed x126, local copies, waits for them, and re-layouts  18 us
    dot_general x5, matrix products, matrix_product(): jnp.dot(left_side.astype(jnp.bfloat16), right_side.astype(jnp.bfloat16),...  12.6 us
    reduce_sum x12, other arithmetic, total(): return jnp.sum(slots.astype(jnp.float32), axis=0)  11.6 us

profile of v3, /device:TPU:0, one launch (start us, length us, event | category | flops | bytes accessed | tf_op | source)
XLA Modules:
  0.0 350.4 jit_solution(11143103750796626464)
XLA Ops:
  0.7 1.5 convert_reduce_fusion.13
  3.0 1.5 copy.196.refs_0_
  4.5 1.5 copy.197.refs_1_
  6.0 1.6 copy.195
  7.7 1.6 constant_dynamic-slice_fusion.2.refs_3_
  9.2 1.6 dynamic-slice_bitcast_fusion.refs_6_
  10.8 1.7 copy.221
  13.5 25.7 %shard_map.347 = (bf16[4,128,192]{2,1,0:T(8,128)(2,1)}, bf16[4,128,192]{2,1,0:T(8,128)(2,1)}, bf16[4,192,192]{2,1,0:T(8,128)(2,1)}) custom-call(bf16[128,192]{1,0:T(8,128)(2,1)} %copy.196.refs_0_, bf16[128,192]{1,0:T(8,128)(2,1)} %copy.197.refs_1_, bf16[192,192]{1,0:T(8,128)(2,1)} %bitcast.260), custom_call_target="tpu_custom_call" | custom-call | tf_op jit(solution)/shard_map/pallas_call | solution.py:100
  41.1 45.8 %shard_map.348 = (bf16[4,512,192]{2,1,0:T(8,128)(2,1)}, bf16[4,128,192]{2,1,0:T(8,128)(2,1)}, f32[4,6,192]{2,1,0:T(8,128)}, bf16[4,96,576]{2,1,0:T(8,128)(2,1)},...) custom-call(bf16[512,192]{1,0:T(8,128)(2,1)} %bitcast.269, ...), custom_call_target="tpu_custom_call" | custom-call | tf_op jit(solution)/shard_map/pallas_call | solution.py:100
  90.4 1.5 fusion.68
  92.8 1.5 subtract_multiply_fusion
  94.3 8.5 %shard_map.349 = (bf16[2,4,96,576]{3,2,1,0:T(8,128)(2,1)}, bf16[2,4,96,768]{3,2,1,0:T(8,128)(2,1)}, bf16[2,4,96,768]{3,2,1,0:T(8,128)(2,1)}, bf16[2,4,96,768]{3,2,1,0:T(8,128)(2,1)}) custom-call(bf16[4,96,576]{2,1,0:T(8,128)(2,1)} %get-tuple-element.64.refs_0_, bf16[4,96,768]{2,1,0:T(8,128)(2,1)} %get-tuple-element.65.refs_1_, ...), custom_call_target="tpu_custom_call" | custom-call | tf_op jit(solution)/shard_map/pallas_call | solution.py:100
  109.0 2.9 fusion.71
  112.5 2.3 fusion.10
  115.8 1.5 copy.246.refs_0_
  117.4 11.4 %shard_map.350 = bf16[4,128,192]{2,1,0:T(8,128)(2,1)} custom-call(bf16[128,192]{1,0:T(8,128)(2,1)} %copy.246.refs_0_), custom_call_target="tpu_custom_call" | custom-call | tf_op jit(solution)/shard_map/pallas_call | solution.py:100
  129.7 2.7 fusion.67
  134.0 1.9 copy.208
  135.9 2.0 copy.209
  137.9 1.9 add_convert_fusion.4
  139.8 1.7 copy.206
  141.6 1.8 copy.207
  143.3 2.1 multiply_convert_fusion.1
  147.1 8.1 %shard_map.351 = bf16[4,32,768]{2,1,0:T(8,128)(2,1)} custom-call(bf16[4,32,768]{2,1,0:T(8,128)(2,1)} %bitcast.261), custom_call_target="tpu_custom_call" | custom-call | tf_op jit(solution)/shard_map/pallas_call | solution.py:100
  158.1 1.6 add_convert_fusion.7.refs_0_
  159.7 8.5 %shard_map.352 = bf16[4,32,768]{2,1,0:T(8,128)(2,1)} custom-call(bf16[32,768]{1,0:T(8,128)(2,1)} %add_convert_fusion.7.refs_0_), custom_call_target="tpu_custom_call" | custom-call | tf_op jit(solution)/shard_map/pallas_call | solution.py:100
  168.2 1.7 convolution_convert_fusion.10
  172.6 34.2 %shard_map.353 = (bf16[4,128,192]{2,1,0:T(8,128)(2,1)}, bf16[4,128,192]{2,1,0:T(8,128)(2,1)}, bf16[4,128,192]{2,1,0:T(8,128)(2,1)}, bf16[4,128,768]{2,1,0:T(8,12...) custom-call(bf16[128,192]{1,0:T(8,128)(2,1)} %copy.210.refs_0_, bf16[4,128,192]{2,1,0:T(8,128)(2,1)} %bitcast.257, ...), custom_call_target="tpu_custom_call" | custom-call | tf_op jit(solution)/shard_map/pallas_call | solution.py:100
  206.7 1.4 convert_reduce_fusion.1
  208.1 2.3 fusion.11.refs_2_
  211.7 1.8 convolution_convert_fusion.9.refs_1_
  215.4 2.6 multiply_convert_fusion
  221.2 2.3 convolution_convert_fusion.1.refs_0_
  224.7 5.3 %shard_map.354 = (bf16[2,192,576]{2,1,0:T(8,128)(2,1)}, bf16[2,192,192]{2,1,0:T(8,128)(2,1)}, bf16[2,192,768]{2,1,0:T(8,128)(2,1)}, bf16[2,768,192]{2,1,0:T(8,128)(2,1)}, f32[2,1,1344]{2,1,0:T(1,128)}) custom-call(bf16[192,576]{1,0:T(8,128)(2,1)} %convolution_convert_fusion.1.refs_0_, bf16[192,192]{1,0:T(8,128)(2,1)} %convolution_convert_fusion.9.refs_1_, ...), custom_call_target="tpu_custom_call" | custom-call | tf_op jit(solution)/shard_map/pallas_call | solution.py:100
  241.0 17.9 %shard_map.355 = (bf16[4,192,384]{2,1,0:T(8,128)(2,1)}, bf16[4,128,192]{2,1,0:T(8,128)(2,1)}, bf16[4,128,192]{2,1,0:T(8,128)(2,1)}) custom-call(bf16[4,192,384]{2,1,0:T(8,128)(2,1)} %fusion.29.refs_0_, bf16[4,128,192]{2,1,0:T(8,128)(2,1)} %bitcast.254, bf16[4,128,192]{2,1,0:T(8,128)(2,1)} %bitcast.255), custom_call_target="tpu_custom_call" | custom-call | tf_op jit(solution)/shard_map/pallas_call | solution.py:100
  266.2 6.8 %shard_map.356 = (f32[4,2,128]{2,1,0:T(2,128)}, f32[4,2,192]{2,1,0:T(2,128)}, bf16[2,768,256]{2,1,0:T(8,128)(2,1)}) custom-call(f32[2,128]{1,0:T(2,128)} %pad_maximum_fusion.8.refs_0_, f32[4,2,192]{2,1,0:T(2,128)} %maximum_bitcast_fusion.1.refs_1_, bf16[2,768,256]{2,1,0:T(8,128)(2,1)} %bitcast.253), custom_call_target="tpu_custom_call" | custom-call | tf_op jit(solution)/shard_map/pallas_call | solution.py:100
  276.9 2.1 reduce_sum.332
  279.1 14.3 %shard_map.357 = (bf16[4,192,256]{2,1,0:T(8,128)(2,1)}, f32[4,6,192]{2,1,0:T(8,128)}) custom-call(bf16[4,192,256]{2,1,0:T(8,128)(2,1)} %bitcast.239, f32[6,192]{1,0:T(8,128)} %stack.79.refs_1_), custom_call_target="tpu_custom_call" | custom-call | tf_op jit(solution)/shard_map/pallas_call | solution.py:100
  293.3 1.7 reduce_sum.338.refs_0_
  295.0 1.4 reduce_sum.339.refs_1_
  296.4 12.2 %shard_map.358 = bf16[4,192,256]{2,1,0:T(8,128)(2,1)} custom-call(bf16[192,256]{1,0:T(8,128)(2,1)} %reduce_sum.338.refs_0_), custom_call_target="tpu_custom_call" | custom-call | tf_op jit(solution)/shard_map/pallas_call | solution.py:100
  308.6 3.7 %shard_map.359 = (bf16[2,768,256]{2,1,0:T(8,128)(2,1)}, f32[2,6,192]{2,1,0:T(8,128)}) custom-call(bf16[768,256]{1,0:T(8,128)(2,1)} %bitcast.240, f32[6,192]{1,0:T(8,128)} %reduce_sum.339.refs_1_), custom_call_target="tpu_custom_call" | custom-call | tf_op jit(solution)/shard_map/pallas_call | solution.py:100
  317.6 2.9 multiply_add_fusion.4
  322.7 2.5 multiply_add_fusion.1
  325.3 4.9 %fusion.9 = bf16[768,384]{1,0:T(8,128)(2,1)} fusion(bf16[768,384]{1,0:T(8,128)(2,1)S(1)} %bitcast.226, f32[768,768]{1,0:T(8,128)S(1)} %multiply_add_fusion.4, f32[768,768]{1,0:T(8,128)} %multiply_add_fusion.1, f32[]{:T(128)S(6)} %rsqrt.35), kind=kOutput, calls=%fused_computation.28 | convolution fusion | flops 1363968000 | bytes 5898244 | tf_op jit(solution)/shard_map/dot_general | solution.py:130
  330.2 11.1 %shard_map.360.refs_0_ = bf16[4,192,384]{2,1,0:T(8,128)(2,1)} custom-call(bf16[4,192,384]{2,1,0:T(8,128)(2,1)} %bitcast.264), custom_call_target="tpu_custom_call" | custom-call | tf_op jit(solution)/shard_map/pallas_call | solution.py:100
  341.3 4.1 %shard_map.361 = bf16[2,4,192,384]{3,2,1,0:T(8,128)(2,1)} custom-call(bf16[4,192,384]{2,1,0:T(8,128)(2,1)} %shard_map.360.refs_0_), custom_call_target="tpu_custom_call" | custom-call | tf_op jit(solution)/shard_map/pallas_call | solution.py:100
  345.4 1.4 slice_bitcast_fusion.1
  (217 shorter events, 65.1 us)
Async XLA Ops:
  0.7 39.6 %copy-start.24 = (bf16[192,768]{1,0:T(8,128)(2,1)S(1)}, bf16[192,768]{1,0:T(8,128)(2,1)}, u32[]{:S(2)}) copy-start(bf16[192,768]{1,0:T(8,128)(2,1)} %param.22) | copy-start | bytes 884740
  86.9 3.4 copy-start.17
  94.3 9.8 %copy-start.9 = (bf16[512,768]{1,0:T(8,128)(2,1)}, bf16[512,768]{1,0:T(8,128)(2,1)S(1)}, u32[]{:S(2)}) copy-start(bf16[512,768]{1,0:T(8,128)(2,1)S(1)} %get-tuple-element.251) | copy-start | bytes 2359300
  94.3 9.8 %copy-start.46 = (f32[576]{0:T(1024)S(1)}, f32[576]{0:T(1024)}, u32[]{:S(2)}) copy-start(f32[576]{0:T(1024)} %param.24) | copy-start | bytes 6916
  104.2 1.3 copy-start.13
  104.9 1.7 copy-start.12
  106.6 1.3 copy-start.11
  143.3 2.1 copy-start.10
  143.3 2.1 copy-start.38
  145.9 1.3 copy-start.23
  145.9 12.2 %copy-start.52 = (f32[32]{0:T(128)S(1)}, f32[32]{0:T(128)}, u32[]{:S(2)}) copy-start(f32[32]{0:T(128)} %dynamic-slice.4) | copy-start | bytes 388
  206.7 3.7 %copy-start = (bf16[4,128,768]{2,1,0:T(8,128)(2,1)S(1)}, bf16[4,128,768]{2,1,0:T(8,128)(2,1)}, u32[]{:S(2)}) copy-start(bf16[4,128,768]{2,1,0:T(8,128)(2,1)} %get-tuple-element.77) | copy-start | bytes 2359300
  206.7 3.7 %copy-start.18 = (bf16[4,128,192]{2,1,0:T(8,128)(2,1)S(1)}, bf16[4,128,192]{2,1,0:T(8,128)(2,1)}, u32[]{:S(2)}) copy-start(bf16[4,128,192]{2,1,0:T(8,128)(2,1)} %get-tuple-element.59.refs_1_) | copy-start | bytes 589828
  218.6 1.3 copy-start.5
  220.3 3.2 copy-start.7
  223.5 8.6 %copy-start.47 = (f32[576]{0:T(1024)S(1)}, f32[576]{0:T(1024)}, u32[]{:S(2)}) copy-start(f32[576]{0:T(1024)} %param.24) | copy-start | bytes 6916
  223.5 8.7 %copy-start.48 = (f32[576]{0:T(1024)S(1)}, f32[576]{0:T(1024)}, u32[]{:S(2)}) copy-start(f32[576]{0:T(1024)} %param.31) | copy-start | bytes 6916
  223.5 9.3 %copy-start.49 = (f32[768]{0:T(1024)S(1)}, f32[768]{0:T(1024)}, u32[]{:S(2)}) copy-start(f32[768]{0:T(1024)} %param.25) | copy-start | bytes 9220
  223.5 9.3 %copy-start.50 = (f32[768]{0:T(1024)S(1)}, f32[768]{0:T(1024)}, u32[]{:S(2)}) copy-start(f32[768]{0:T(1024)} %param.32) | copy-start | bytes 9220
  223.8 10.7 %copy-start.22 = (f32[192,192]{0,1:T(8,128)S(1)}, f32[192,192]{0,1:T(8,128)}, u32[]{:S(2)}) copy-start(f32[192,192]{0,1:T(8,128)} %copy.221) | copy-start | bytes 442372
  230.0 5.4 %copy-start.26 = (bf16[2,192,768]{2,1,0:T(8,128)(2,1)S(1)}, bf16[2,192,768]{2,1,0:T(8,128)(2,1)}, u32[]{:S(2)}) copy-start(bf16[2,192,768]{2,1,0:T(8,128)(2,1)} %get-tuple-element.80) | copy-start | bytes 1769476
  231.2 4.3 %copy-start.4 = (f32[192,576]{1,0:T(8,128)}, f32[192,576]{1,0:T(8,128)S(1)}, u32[]{:S(2)}) copy-start(f32[192,576]{1,0:T(8,128)S(1)} %convert_reduce_fusion.5) | copy-start | bytes 1327108
  232.1 3.4 copy-start.41
  232.1 3.4 copy-start.42
  235.4 1.3 copy-start.20
  235.5 3.2 copy-start.2
  237.8 2.4 copy-start.3
  237.8 1.5 copy-start.28
  258.9 5.5 %copy-start.1 = (bf16[4,192,384]{2,1,0:T(8,128)(2,1)S(1)}, bf16[4,192,384]{2,1,0:T(8,128)(2,1)}, u32[]{:S(2)}) copy-start(bf16[4,192,384]{2,1,0:T(8,128)(2,1)} %get-tuple-element.84) | copy-start | bytes 1769476
  265.2 8.5 %copy-start.53 = (f32[128]{0:T(128)S(1)}, f32[128]{0:T(128)}, u32[]{:S(2)}) copy-start(f32[128]{0:T(128)} %dynamic-slice.5) | copy-start | bytes 1540
  265.2 10.4 %copy-start.45 = (f32[192]{0:T(256)S(1)}, f32[192]{0:T(256)}, u32[]{:S(2)}) copy-start(f32[192]{0:T(256)} %convert_reduce_fusion.13) | copy-start | bytes 2308
  276.9 36.1 %copy-start.39 = (f32[6,192]{1,0:T(8,128)S(1)}, f32[6,192]{1,0:T(8,128)}, u32[]{:S(2)}) copy-start(f32[6,192]{1,0:T(8,128)} %refs_2_.1) | copy-start | bytes 13828
  276.9 36.1 %copy-start.44 = (f32[6,192]{1,0:T(8,128)S(1)}, f32[6,192]{1,0:T(8,128)}, u32[]{:S(2)}) copy-start(f32[6,192]{1,0:T(8,128)} %param.33) | copy-start | bytes 13828
  313.0 2.4 copy-start.40
  314.9 1.9 copy-start.31
  314.9 1.9 copy-start.33
  314.9 1.9 copy-start.35
  315.2 1.7 copy-start.29
  315.4 2.1 copy-start.14
  317.5 2.9 copy-start.15
  317.5 2.9 copy-start.30
  317.5 2.9 copy-start.32
  317.5 2.9 copy-start.34
  317.5 2.9 copy-start.36
  345.4 1.4 copy-start.19
  345.4 2.3 copy-start.8
  346.8 1.7 copy-start.25
  347.7 1.7 copy-start.6
  (6 other events, 5.2 us)
